TPU v7x, 32 devices: a whole 2x2x4 slice. The times are simulated.
32 devices in a mesh: pair: 8 (over z, y), band: 4 (over x, core).
Axes of the slice: x: 2, y: 2, z: 4, core: 2. Of those that a mesh axis runs over, the one named last changes fastest.
Arguments:
- orbitals: bfloat16 [2048, 23, 64], P('pair'), may hold values from -6 to 6
- screening: bfloat16 [1024, 8, 1024], P('pair', None, 'band'), may hold values from -0.1875 to 0.1875
- trial: bfloat16 [1024, 23, 64], P('pair'), may hold values from -6 to 6
- pair_kpts: int32 [8, 2], replicated, may hold values from 0 to 22
- pair_q: int32 [8], replicated, may hold values from 0 to 7
Outputs:
- applied: float32 [1024, 23, 64], P('pair', None, 'band')
All inputs are finite; a program needn't handle non-finite values.
Results may differ from a plain program's by a relative error of at most 0.013.
Values may be sent and summed in bfloat16 or wider, within the bound.
No kernel may reach another device: no remote copies, remote signals or barrier semaphores. Data moves between devices by JAX's collectives and lax.ppermute only.
A program may use at most 64 MiB of HBM per device.

v0:
```python
import math

import jax
import jax.numpy as jnp
from jax import lax
from jax.sharding import PartitionSpec as P

NV = 32
NC = 32
NR = 2048
NG = 1024
KPTS = 23
NB = 64


def basis_rows(first_row, row_count, point_count):
    frequency = first_row + jnp.arange(row_count, dtype=jnp.int32)
    position = jnp.arange(point_count, dtype=jnp.int32)
    phase_index = (2 * position[None, :] + 1) * frequency[:, None] % (4 * point_count)
    values = jnp.cos(phase_index.astype(jnp.float32) * (math.pi / (2 * point_count))) * math.sqrt(
        2.0 / point_count
    )
    return values.astype(jnp.bfloat16)


def densities(first_set, second_set):
    merged = first_set.astype(jnp.float32)[:, :, None] * second_set.astype(jnp.float32)[:, None, :]
    return merged.reshape(first_set.shape[0], first_set.shape[1] * second_set.shape[1]).astype(
        jnp.bfloat16
    )


def transform(basis_block, first_set, second_set):
    return lax.dot_general(
        basis_block,
        densities(first_set, second_set),
        (((1,), (0,)), ((), ())),
        preferred_element_type=jnp.float32,
    ).astype(jnp.bfloat16)


def on_device(orbitals, screening, trial, pair_kpts, pair_q):
    band_count = lax.axis_size("band")
    pair_count = lax.axis_size("pair")
    pair_here = lax.axis_index("pair")
    own_kpts = lax.dynamic_index_in_dim(pair_kpts, pair_here, 0, keepdims=False)
    listed = pair_kpts.shape[0]
    vector_count = trial.shape[2]
    orbital_send = orbitals[:, pair_kpts].reshape(orbitals.shape[0], listed, 2 * NB)
    trial_send = trial[:, pair_kpts].reshape(trial.shape[0], listed, 2 * vector_count)
    screen_send = screening[:, pair_q]
    orbital_got, trial_got, screen_got = (
        lax.all_to_all(orbital_send, "pair", split_axis=1, concat_axis=0, tiled=True),
        lax.all_to_all(trial_send, "pair", split_axis=1, concat_axis=0, tiled=True),
        lax.all_to_all(screen_send, "pair", split_axis=1, concat_axis=0, tiled=True),
    )
    screen_cols = screen_got[:, 0]
    first_orb = orbital_got[:, 0, :NB]
    second_orb = orbital_got[:, 0, NB:]
    row_count = NG // band_count
    basis_block = basis_rows(lax.axis_index("band") * row_count, row_count, NR)
    valence = transform(basis_block, first_orb[:, :NV], second_orb[:, :NV])
    conduction = transform(basis_block, first_orb[:, NV:], second_orb[:, NV:])
    screened = lax.dot_general(
        screen_cols,
        lax.all_gather(valence, "band", axis=0, tiled=True),
        (((0,), (0,)), ((), ())),
        preferred_element_type=jnp.float32,
    ).astype(jnp.bfloat16)
    raw = lax.dot_general(
        conduction, screened, (((0,), (0,)), ((), ())), preferred_element_type=jnp.float32
    ) * (1.0 / math.sqrt(NG))
    kernel = (
        raw.reshape(NC, NC, NV, NV)
        .transpose(2, 0, 3, 1)
        .reshape(NV * NC, NV * NC)
        .astype(jnp.bfloat16)
    )
    trial_first = trial_got[:, 0, :vector_count]
    trial_second = trial_got[:, 0, vector_count:]
    apply_scale = 1.0 / math.sqrt(NV * NC)
    forward = (
        lax.dot_general(
            kernel, trial_second, (((1,), (0,)), ((), ())), preferred_element_type=jnp.float32
        )
        * apply_scale
    )
    backward = (
        lax.dot_general(
            kernel, trial_first, (((0,), (0,)), ((), ())), preferred_element_type=jnp.float32
        )
        * apply_scale
    )
    partials = jnp.stack([forward, backward])
    summed = lax.psum_scatter(
        partials.astype(jnp.bfloat16), "band", scatter_dimension=2, tiled=True
    ).astype(jnp.float32)
    share = summed.shape[2]
    state_rows = summed.shape[1] // pair_count
    kpt_ids = jnp.arange(KPTS, dtype=jnp.int32)
    one_hot = (own_kpts[:, None] == kpt_ids[None, :]).astype(jnp.float32)
    spread = (
        summed[0][:, None, :] * one_hot[0][None, :, None]
        + summed[1][:, None, :] * one_hot[1][None, :, None]
    )
    spread = spread.reshape(summed.shape[1], KPTS * share)
    scattered = lax.psum_scatter(spread, "pair", scatter_dimension=0, tiled=True)
    return scattered.reshape(state_rows, KPTS, share)


def solution(mesh):
    return jax.shard_map(
        on_device,
        mesh=mesh,
        in_specs=(P("pair", None, None), P("pair", None, "band"), P("pair", None, None), P(), P()),
        out_specs=P("pair", None, "band"),
        check_vma=False,
    )
```

profile of v0, /device:TPU:0, one launch (start us, length us, event | category | flops | bytes accessed | tf_op | source)
XLA Modules:
  0.0 212.1 jit_solution(7176523066295668518)
XLA Ops:
  6.5 0.8 compare_select_fusion
  7.5 0.2 copy-done
  7.7 1.4 gather_fusion
  9.1 7.3 %all-to-all-start = ((bf16[256,8,128]{0,2,1:T(8,128)(2,1)}), bf16[256,8,128]{0,2,1:T(8,128)(2,1)S(1)}, u32[]{:S(2)}, u32[]{:S(2)}) async-start(bf16[256,8,128]{0,2,1:T(8,128)(2,1)} %bitcast.2), calls=%async_computation | async-start | bytes 1048576 | tf_op jit(solution)/shard_map/all_to_all | solution.py:53
  16.4 14.4 %all-to-all-done = bf16[256,8,128]{0,2,1:T(8,128)(2,1)S(1)} async-done(((bf16[256,8,128]{0,2,1:T(8,128)(2,1)}), bf16[256,8,128]{0,2,1:T(8,128)(2,1)S(1)}, u32[]{:S(2)}, u32[]{:S(2)}) %all-to-all-start) | async-done | bytes 524320 | tf_op jit(solution)/shard_map/all_to_all | solution.py:53
  30.9 0.3 copy.26
  31.1 0.2 fusion.23
  31.3 0.2 copy.28
  31.6 0.2 copy.27
  31.8 4.2 %multiply_convert_fusion = (bf16[2048,32,32]{0,2,1:T(8,128)(2,1)S(1)}, bf16[2048,32,32]{0,2,1:T(8,128)(2,1)}) fusion(f32[2048,32]{0,1:T(8,128)S(1)} %get-tuple-element.9, f32[2048,32]{0,1:T(8,128)S(1)} %get-tuple-element.7, f32[2048,32]{0,1:T(8,128)S(1)} %get-tuple-element.10, f32[2048,32]{0,1:T(8,128)S(1)} %get-tuple-element.8), kind=kLoop, calls=%fused_computation.3 | loop fusion | flops 8388608 | bytes 9437184 | tf_op jit(solution)/shard_map/convert_element_type | solution.py:28
  36.0 10.2 %convolution_convert_fusion.1 = bf16[256,1024]{1,0:T(8,128)(2,1)} fusion(bf16[2048,1024]{0,1:T(8,128)(2,1)S(1)} %bitcast.70, s32[256]{0:T(256)S(1)} %iota_add_fusion, s32[2048]{0:T(1024)S(1)} %multiply_add_fusion), kind=kOutput, calls=%fused_computation.21 | convolution fusion | flops 1082392576 | bytes 4727808 | tf_op jit(solution)/shard_map/dot_general | solution.py:34
  46.3 1.3 gather_fusion.2
  47.6 3.6 %all-to-all-start.2 = ((bf16[128,8,128]{0,2,1:T(8,128)(2,1)}), bf16[128,8,128]{0,2,1:T(8,128)(2,1)S(1)}, u32[]{:S(2)}, u32[]{:S(2)}) async-start(bf16[128,8,128]{0,2,1:T(8,128)(2,1)} %bitcast.17), calls=%async_computation.2 | async-start | bytes 524288 | tf_op jit(solution)/shard_map/all_to_all | solution.py:54
  51.3 2.0 gather_fusion.1
  53.3 0.9 copy.29
  54.2 6.1 %all-to-all-done.2 = bf16[128,8,128]{0,2,1:T(8,128)(2,1)S(1)} async-done(((bf16[128,8,128]{0,2,1:T(8,128)(2,1)}), bf16[128,8,128]{0,2,1:T(8,128)(2,1)S(1)}, u32[]{:S(2)}, u32[]{:S(2)}) %all-to-all-start.2) | async-done | bytes 262176 | tf_op jit(solution)/shard_map/all_to_all | solution.py:54
  60.3 3.6 %all-to-all-start.1 = ((bf16[128,8,256]{2,0,1:T(8,128)(2,1)}), bf16[128,8,256]{2,0,1:T(8,128)(2,1)S(1)}, u32[]{:S(2)}, u32[]{:S(2)}) async-start(bf16[128,8,256]{2,0,1:T(8,128)(2,1)} %copy.29), calls=%async_computation.1 | async-start | bytes 1048576 | tf_op jit(solution)/shard_map/all_to_all | solution.py:55
  63.9 0.2 reduce-scatter.3.cloned.1.call-start
  64.3 11.5 %convolution_convert_fusion.2 = bf16[256,1024]{1,0:T(8,128)(2,1)} fusion(bf16[2048,1024]{0,1:T(8,128)(2,1)} %bitcast.69, s32[256]{0:T(256)S(1)} %iota_add_fusion, s32[2048]{0:T(1024)S(1)} %multiply_add_fusion), kind=kOutput, calls=%fused_computation.22 | convolution fusion | flops 1082392576 | bytes 4727808 | tf_op jit(solution)/shard_map/dot_general | solution.py:34
  75.8 2.3 %all-to-all-done.1 = bf16[128,8,256]{2,0,1:T(8,128)(2,1)S(1)} async-done(((bf16[128,8,256]{2,0,1:T(8,128)(2,1)}), bf16[128,8,256]{2,0,1:T(8,128)(2,1)S(1)}, u32[]{:S(2)}, u32[]{:S(2)}) %all-to-all-start.1) | async-done | bytes 524320 | tf_op jit(solution)/shard_map/all_to_all | solution.py:55
  78.1 0.8 copy-done.3
  78.9 3.3 %multiply_convert_fusion.2 = bf16[1024,1024]{1,0:T(8,128)(2,1)S(1)} fusion(bf16[256,1024]{1,0:T(8,128)(2,1)} %convolution_convert_fusion.2, bf16[1024,256]{1,0:T(8,128)(2,1)} %bitcast.78, bf16[1024,1024]{1,0:T(8,128)(2,1)} %all-gather.2.cloned.1.call-done), kind=kOutput, calls=%fused_computation.5 | convolution fusion | flops 1076101120 | bytes 5242880 | tf_op jit(solution)/shard_map/dot_general | solution.py:70
  82.2 8.2 %convert_element_type.73 = bf16[32,32,32,32]{3,2,1,0:T(8,128)(2,1)} reshape(bf16[1024,1024]{1,0:T(8,128)(2,1)S(1)} %multiply_convert_fusion.2) | data formatting | bytes 4194304 | tf_op jit(solution)/shard_map/convert_element_type | solution.py:77
  90.4 15.2 %copy.30 = bf16[32,32,32,32]{1,3,0,2:T(8,128)(2,1)} copy(bf16[32,32,32,32]{3,2,1,0:T(8,128)(2,1)} %convert_element_type.73) | data formatting | bytes 4194304 | tf_op jit(solution)/shard_map/convert_element_type | solution.py:77
  105.6 11.3 %convert_element_type.75 = bf16[1024,1024]{1,0:T(8,128)(2,1)S(1)} reshape(bf16[32,32,32,32]{3,2,1,0:T(8,128)(2,1)} %bitcast.67) | data formatting | bytes 4194304 | tf_op jit(solution)/shard_map/convert_element_type | solution.py:77
  116.9 0.8 fusion.10
  117.8 0.5 fusion.9
  118.3 0.7 pad_maximum_fusion
  119.7 18.6 %reduce-scatter.3.cloned.1.call-done = bf16[2,1024,16]{1,2,0:T(8,128)(2,1)} async-done(((bf16[2,1024,64]{1,2,0:T(8,128)(2,1)}), bf16[2,1024,16]{1,2,0:T(8,128)(2,1)}) %reduce-scatter.3.cloned.1.call-update) | async-done | bytes 65552 | tf_op jit(solution)/shard_map/reduce_scatter | solution.py:95
  138.3 0.8 convert_element_type.76
  139.2 1.4 fusion.6
  140.6 65.0 %reduce-scatter.5.cloned.1.call-done = f32[128,368]{0,1:T(8,128)} async-done(((f32[1024,368]{0,1:T(8,128)}), f32[128,368]{0,1:T(8,128)}) %reduce-scatter.5.cloned.1.call-update) | async-done | bytes 188432 | tf_op jit(solution)/shard_map/reduce_scatter | solution.py:107
  (34 shorter events, 1.2 us)
Async XLA Ops:
  6.5 1.1 copy-start
  9.1 21.8 %all-to-all-start = ((bf16[256,8,128]{0,2,1:T(8,128)(2,1)}), bf16[256,8,128]{0,2,1:T(8,128)(2,1)S(1)}, u32[]{:S(2)}, u32[]{:S(2)}) async-start(bf16[256,8,128]{0,2,1:T(8,128)(2,1)} %bitcast.2), calls=%async_computation | async-start | bytes 1048576 | tf_op jit(solution)/shard_map/all_to_all | solution.py:53
  16.4 61.8 %all-gather.2.cloned.1.call-start = ((), (), s32[]{:S(2)}) async-start(), calls=%async_computation.5 | async-start | bytes 2621440 | tf_op jit(solution)/shard_map/all_gather | solution.py:66
  36.0 10.2 %copy-start.2 = (bf16[128,23,64]{0,2,1:T(8,128)(2,1)S(1)}, bf16[128,23,64]{0,2,1:T(8,128)(2,1)}, u32[]{:S(2)}) copy-start(bf16[128,23,64]{0,2,1:T(8,128)(2,1)} %param.7) | copy-start | bytes 1130500
  46.2 5.0 %copy-start.5 = (s32[8]{0:T(128)S(1)}, s32[8]{0:T(128)}, u32[]{:S(2)}) copy-start(s32[8]{0:T(128)} %param.9) | copy-start | bytes 100
  46.2 5.0 %copy-start.1 = (bf16[128,8,256]{2,1,0:T(8,128)(2,1)S(1)}, bf16[128,8,256]{2,1,0:T(8,128)(2,1)}, u32[]{:S(2)}) copy-start(bf16[128,8,256]{2,1,0:T(8,128)(2,1)} %param.6) | copy-start | bytes 1572868
  47.6 12.7 %all-to-all-start.2 = ((bf16[128,8,128]{0,2,1:T(8,128)(2,1)}), bf16[128,8,128]{0,2,1:T(8,128)(2,1)S(1)}, u32[]{:S(2)}, u32[]{:S(2)}) async-start(bf16[128,8,128]{0,2,1:T(8,128)(2,1)} %bitcast.17), calls=%async_computation.2 | async-start | bytes 524288 | tf_op jit(solution)/shard_map/all_to_all | solution.py:54
  60.3 17.8 %all-to-all-start.1 = ((bf16[128,8,256]{2,0,1:T(8,128)(2,1)}), bf16[128,8,256]{2,0,1:T(8,128)(2,1)S(1)}, u32[]{:S(2)}, u32[]{:S(2)}) async-start(bf16[128,8,256]{2,0,1:T(8,128)(2,1)} %copy.29), calls=%async_computation.1 | async-start | bytes 1048576 | tf_op jit(solution)/shard_map/all_to_all | solution.py:55
  63.9 74.4 %reduce-scatter.3.cloned.1.call-start = ((), (), s32[]{:S(2)}) async-start(), calls=%async_computation.6 | async-start | bytes 327680 | tf_op jit(solution)/shard_map/reduce_scatter | solution.py:95
  78.1 0.8 copy-start.3
  117.7 1.3 copy-start.4
  119.0 86.5 %reduce-scatter.5.cloned.1.call-start = ((), (), s32[]{:S(2)}) async-start(), calls=%async_computation.7 | async-start | bytes 1695744 | tf_op jit(solution)/shard_map/reduce_scatter | solution.py:107
Sparse Core Ops, SparseCore 0:
  46.4 21.6 all-gather.1
  119.1 19.1 reduce-scatter.2
  141.7 63.7 reduce-scatter.4
where the time goes:
time: 213 us; the launch traced here: 212 us
  waiting for transfers between devices  106 us (50%)
  local copies, waits for them, and re-layouts  43.1 us (20%)
  matrix products  26.3 us (12%)
  starting transfers between devices  14.8 us (7%)
  between operations  13.3 us (6%)
  other arithmetic  8.09 us (4%)
    reduce_scatter x1, waiting for transfers between devices, on_device(): lax.psum_scatter(spread, 'pair', scatter_dimension=0, tiled=True)  65 us
    convert_element_type x3, local copies, waits for them, and re-layouts, on_device(): kernel = raw.reshape(NC, NC, NV, NV).transpose(2, 0, 3, 1).reshape(NV * N...  34.7 us
    dot_general x2, matrix products, transform(): lax.dot_general(basis_block, densities(first_set, second_set), (((1,), (0...  21.7 us
    reduce_scatter x1, waiting for transfers between devices, on_device(): lax.psum_scatter(partials.astype(jnp.bfloat16), 'band', scatter_dimension...  18.6 us
    all_to_all x1, waiting for transfers between devices, on_device(): lax.all_to_all(orbital_send, 'pair', split_axis=1, concat_axis=0, tiled=T...  14.4 us
    all_to_all x1, starting transfers between devices, on_device(): lax.all_to_all(orbital_send, 'pair', split_axis=1, concat_axis=0, tiled=T...  7.31 us
    all_to_all x1, waiting for transfers between devices, on_device(): lax.all_to_all(trial_send, 'pair', split_axis=1, concat_axis=0, tiled=True)  6.1 us
  transfers between devices with their start and end apart: 6, of which 5 were waited for; matrix products, arithmetic and copies ran while one was open for 8% of the time, Pallas kernels for 0%

commit v1 on v0

v1 whole, which is shorter than its diff:
```python
import math

import jax
import jax.numpy as jnp
from jax import lax
from jax.experimental import pallas as pl
from jax.experimental.pallas import tpu as pltpu
from jax.sharding import Mesh, PartitionSpec as P

NV = 32
NC = 32
NR = 2048
NG = 1024
NB = 64
NVC = NV * NC
HALVES = 2
TABLE = 64
F32 = jnp.float32
BF16 = jnp.bfloat16
VMEM_LIMIT = 56 * 1024 * 1024


def dot(a, b):
    return lax.dot_general(a, b, (((1,), (0,)), ((), ())), preferred_element_type=F32)


def dot_rows(a, b):
    return lax.dot_general(a, b, (((1,), (1,)), ((), ())), preferred_element_type=F32)


def call(body, out, scratch=(), smem=0, cost=None, name=None, args=0):
    many = isinstance(out, (list, tuple))
    specs = [pl.BlockSpec(memory_space=pltpu.SMEM)] * smem + [
        pl.BlockSpec(memory_space=pltpu.VMEM)
    ] * (args - smem)
    return pl.pallas_call(
        body,
        out_shape=out,
        in_specs=specs,
        scratch_shapes=list(scratch),
        compiler_params=pltpu.CompilerParams(vmem_limit_bytes=VMEM_LIMIT),
        cost_estimate=cost,
        name=name,
    )


def cost(flops, moved):
    return pl.CostEstimate(flops=int(flops), transcendentals=0, bytes_accessed=int(moved))


def basis_kernel(out_ref, cos_low, sin_low, cos_high, sin_high):
    columns = out_ref.shape[1]
    half = columns // 2
    groups = lax.axis_size("bc")
    strip = NG // (lax.axis_size("bx") * groups)
    column = lax.broadcasted_iota(jnp.int32, (1, columns), 1)
    inner = column - half
    frequency = jnp.where(
        column < half,
        lax.axis_index("ph") * half + column,
        (inner // strip * groups + lax.axis_index("bc")) * strip + inner % strip,
    )
    period = 4 * NR
    unit = math.pi / (2 * NR)

    def angle(index):
        index = index & (period - 1)
        return jnp.where(index >= period // 2, index - period, index).astype(F32) * unit

    low = lax.broadcasted_iota(jnp.int32, (TABLE, columns), 0)
    low_angle = angle((2 * low + 1) * frequency)
    scale = math.sqrt(2.0 / NR)
    cos_low[...] = jnp.cos(low_angle) * scale
    sin_low[...] = jnp.sin(low_angle) * scale
    high = lax.broadcasted_iota(jnp.int32, (NR // TABLE, columns), 0)
    high_angle = angle(2 * TABLE * high * frequency)
    cos_high[...] = jnp.cos(high_angle)
    sin_high[...] = jnp.sin(high_angle)

    def step(block, carry):
        value = cos_low[...] * cos_high[pl.ds(block, 1), :] - sin_low[...] * sin_high[pl.ds(block, 1), :]
        out_ref[pl.ds(pl.multiple_of(block * TABLE, TABLE), TABLE), :] = value.astype(BF16)
        return carry

    lax.fori_loop(0, NR // TABLE, step, 0)


def transform_kernel(
    own_ref, other_ref, basis_ref, val_ref, cond_ref, swap_ref, first, second, density, wide
):
    side = lax.axis_index("bc")
    blocks, bands, _ = own_ref.shape
    points = NR // blocks
    for b in range(blocks):
        where = slice(b * points, (b + 1) * points)
        own = own_ref[b, :, :points].astype(F32)
        other = other_ref[b, :, :points].astype(F32)
        first[side, :, where] = own[:NV]
        second[side, :, where] = own[NV:]
        first[1 - side, :, where] = other[:NV]
        second[1 - side, :, where] = other[NV:]
    chunk = 8
    half = val_ref.shape[1]
    for kind in range(2):

        def step(i, carry):
            right = second[kind]
            for j in range(chunk):
                left = first[kind, pl.ds(i * chunk + j, 1), :]
                density[j * NV : (j + 1) * NV, :] = (left * right).astype(BF16)
            rows = pl.ds(pl.multiple_of(i * chunk * NV, chunk * NV), chunk * NV)
            result = dot(density[...], basis_ref[:, kind * half : (kind + 1) * half])
            if kind == 0:
                val_ref[rows, :] = result.astype(BF16)
            else:
                cond_ref[rows, :] = result.astype(BF16)
                for t in range(half // 128):
                    wide[t, rows, :] = result[:, t * 128 : (t + 1) * 128]
            return carry

        lax.fori_loop(0, NV // chunk, step, 0)

    def swap(d, carry):
        for t in range(half // 128):
            swap_ref[pl.ds(pl.multiple_of(d * NC, NC), NC), t * 128 : (t + 1) * 128] = wide[
                t, pl.ds(d, NC, stride=NC), :
            ].astype(BF16)
        return carry

    lax.fori_loop(0, NC, swap, 0)


def apply_kernel(
    own_ref,
    other_ref,
    val_ref,
    screen_ref,
    cond_ref,
    swap_ref,
    out_ref,
    screen,
    wide,
    screened,
    slabs,
    vectors,
    diagonal,
    sides,
):
    side = lax.axis_index("bc")
    blocks, count, width = own_ref.shape
    states = NVC // blocks
    half = val_ref.shape[1]
    strips = lax.axis_size("bx")
    tall = screen_ref.shape[1]
    broad = screen_ref.shape[2]
    for b in range(screen_ref.shape[0]):
        row, col = b // strips, b % strips
        screen[row * tall : (row + 1) * tall, col * broad : (col + 1) * broad] = screen_ref[b]
    chunk = 256

    def screen_step(i, carry):
        rows = pl.ds(pl.multiple_of(i * chunk, chunk), chunk)
        result = dot(val_ref[rows, :], screen[...])
        for t in range(half // 128):
            wide[t, rows, :] = result[:, t * 128 : (t + 1) * 128]
        screened[0, rows, :] = result.astype(BF16)
        return carry

    lax.fori_loop(0, NVC // chunk, screen_step, 0)

    def swap(w, carry):
        for t in range(half // 128):
            screened[1, pl.ds(pl.multiple_of(w * NV, NV), NV), t * 128 : (t + 1) * 128] = wide[
                t, pl.ds(w, NV, stride=NV), :
            ].astype(BF16)
        return carry

    lax.fori_loop(0, NV, swap, 0)

    repeat = 128 // NV
    lanes = repeat * count
    for b in range(blocks):
        where = slice(b * states, (b + 1) * states)
        for slot, ref in ((side, own_ref), (1 - side, other_ref)):
            turned = ref[b, :, width - states :].astype(F32).T
            vectors[slot, where, :] = jnp.concatenate([turned] * (128 // count), axis=1)
    lane = lax.broadcasted_iota(jnp.int32, (NV, lanes), 1) // count
    per = chunk // NC
    groups = NVC // 128
    total = apply_scale() * (1.0 / math.sqrt(NG))
    for kind in range(2):
        left_ref = swap_ref if kind == 0 else cond_ref

        def spread(d, carry):
            rows = vectors[1 - kind, pl.ds(d, NV, stride=NV), :]
            rows = jnp.concatenate([rows] * (lanes // 128), axis=1)
            for r in range(repeat):
                diagonal[pl.ds(pl.multiple_of(d * 128 + r * NV, NV), NV), :] = jnp.where(
                    lane == r, rows, 0.0
                ).astype(BF16)
            return carry

        lax.fori_loop(0, NC, spread, 0)

        def raw_step(i, carry):
            rows = pl.ds(pl.multiple_of(i * chunk, chunk), chunk)
            raw = dot_rows(left_ref[rows, :], screened[kind]).astype(BF16)
            for j in range(per):
                for g in range(groups):
                    slabs[i, g * NC : (g + 1) * NC, j * 128 : (j + 1) * 128] = raw[
                        j * NC : (j + 1) * NC, g * 128 : (g + 1) * 128
                    ]
            return carry

        lax.fori_loop(0, NVC // chunk, raw_step, 0)
        sides[...] = jnp.zeros_like(sides)

        def sum_step(i, carry):
            rows = pl.ds(pl.multiple_of(i * per * 128, per * 128), per * 128)
            sides[...] += dot(slabs[i], diagonal[rows, :])
            return carry

        lax.fori_loop(0, NVC // chunk, sum_step, 0)
        for g in range(groups):
            block = sides[g * NC : (g + 1) * NC, :] * total
            stacked = jnp.concatenate([block[:, r * count : (r + 1) * count] for r in range(repeat)], axis=0)
            out_ref[kind, :, g * 128 : (g + 1) * 128] = stacked.T.astype(BF16)


def apply_scale():
    return 1.0 / math.sqrt(NVC)


def gather_kernel(kpts_ref, got_ref, out_ref):
    pairs_low = lax.axis_size("bx")
    out_ref[...] = jnp.zeros_like(out_ref)
    halves, low, strips, groups = got_ref.shape[:4]
    for p in range(low * strips):
        for s in range(2):
            total = None
            for h in range(halves):
                for g in range(groups):
                    part = got_ref[h, p // strips, p % strips, g, s].astype(F32)
                    total = part if total is None else total + part
            k = kpts_ref[p, s]
            out_ref[k] += total


def on_device(orbitals, screening, trial, pair_kpts, pair_q):
    halves, low, strips, groups = (lax.axis_size(a) for a in ("ph", "pl", "bx", "bc"))
    pair_axes, all_axes = ("ph", "pl"), ("ph", "pl", "bx", "bc")
    pair_count = halves * low
    points, kpt_count, _ = orbitals.shape
    states, _, count = trial.shape
    bx, bc = lax.axis_index("bx"), lax.axis_index("bc")
    half = NG // HALVES

    near = lax.dynamic_index_in_dim(pair_kpts.reshape(low, strips, 2), bx, 1, keepdims=False)
    orbital_t = lax.dynamic_slice_in_dim(orbitals.transpose(1, 2, 0), bc * NV, NV, 1)
    orbital_part = orbital_t[near].reshape(low, 2 * NV, points)
    which = lax.dynamic_index_in_dim(near, bc, 1, keepdims=False)
    trial_part = trial.transpose(1, 2, 0)[which]
    send = jnp.concatenate([orbital_part, trial_part], axis=2)
    send = jnp.concatenate([send] * halves, axis=0)
    got = lax.all_to_all(send, pair_axes, split_axis=0, concat_axis=0, tiled=True)

    screen_send = screening.transpose(1, 0, 2)[pair_q]
    screen_got = lax.all_to_all(screen_send, ("pl", "bx"), split_axis=0, concat_axis=0, tiled=True)
    swap = [(i, i ^ 1) for i in range(groups)]
    other = lax.ppermute(got, "bc", swap)

    if points % 128 or states % 128:

        def joined(x):
            turned = x.transpose(1, 0, 2)
            return jnp.concatenate(
                [
                    turned[:, :, :points].reshape(1, x.shape[1], pair_count * points),
                    turned[:, :, points:].reshape(1, x.shape[1], pair_count * states),
                ],
                axis=2,
            )

        got, other = joined(got), joined(other)
        tall, broad = screen_got.shape[1:]
        screen_got = screen_got.reshape(low, strips, tall, broad).transpose(1, 0, 2, 3)
        screen_got = screen_got.reshape(strips, low * tall, broad)

    basis = call(
        basis_kernel,
        jax.ShapeDtypeStruct((NR, 2 * half), BF16),
        [pltpu.VMEM((TABLE, 2 * half), F32)] * 2 + [pltpu.VMEM((NR // TABLE, 2 * half), F32)] * 2,
        cost=cost(NR * NG * 4, NR * NG * 2),
        name="basis",
    )()
    valence, conduction, swapped = call(
        transform_kernel,
        [jax.ShapeDtypeStruct((NVC, half), BF16)] * 3,
        [
            pltpu.VMEM((2, NV, NR), F32),
            pltpu.VMEM((2, NV, NR), F32),
            pltpu.VMEM((8 * NV, NR), BF16),
            pltpu.VMEM((half // 128, NVC, 128), F32),
        ],
        cost=cost(2 * NVC * NR * half * 2, NR * NG * 2),
        name="transform",
        args=3,
    )(got, other, basis)
    partial = call(
        apply_kernel,
        jax.ShapeDtypeStruct((2, count, NVC), BF16),
        [
            pltpu.VMEM((half, half), BF16),
            pltpu.VMEM((half // 128, NVC, 128), F32),
            pltpu.VMEM((2, NVC, half), BF16),
            pltpu.VMEM((4, 2 * NVC // 8, 8 * 128), BF16),
            pltpu.VMEM((2, NVC, 128), F32),
            pltpu.VMEM((NC * 128, 4 * count), BF16),
            pltpu.VMEM((8 * NC, 4 * count), F32),
        ],
        cost=cost(2 * NVC * half * half + 8 * NVC * NVC * half, NVC * NVC),
        name="apply",
        args=6,
    )(got, other, valence, screen_got, conduction, swapped)

    share = count // (strips * groups)
    out_send = partial.reshape(2, strips * groups, share, pair_count, states)
    out_send = out_send.transpose(3, 1, 0, 2, 4).reshape(pair_count * strips * groups, 2, share, states)
    out_got = lax.all_to_all(out_send, all_axes, split_axis=0, concat_axis=0, tiled=True)
    out_got = out_got.reshape(halves, low, strips, groups, 2, share, states)
    if states % 128:
        summed = jnp.sum(out_got.astype(F32), axis=(0, 3)).reshape(-1, share * states)
        hot = (pair_kpts.reshape(-1)[None, :] == jnp.arange(kpt_count)[:, None]).astype(F32)
        applied = lax.dot_general(
            hot, summed, (((1,), (0,)), ((), ())), precision=lax.Precision.HIGHEST, preferred_element_type=F32
        ).reshape(kpt_count, share, states)
    else:
        applied = call(
            gather_kernel,
            jax.ShapeDtypeStruct((kpt_count, share, states), F32),
            smem=1,
            name="gather",
            args=2,
        )(pair_kpts, out_got)
    return applied.transpose(2, 0, 1)


def solution(mesh):
    pair_count, band_count = mesh.shape["pair"], mesh.shape["band"]
    shape = (HALVES, pair_count // HALVES, 2, band_count // 2)
    fine = Mesh(mesh.devices.reshape(shape), ("ph", "pl", "bx", "bc"))
    pair_axes, band_axes = ("ph", "pl"), ("bx", "bc")
    return jax.shard_map(
        on_device,
        mesh=fine,
        in_specs=(
            P(pair_axes, None, None),
            P(pair_axes, None, band_axes),
            P(pair_axes, None, None),
            P(),
            P(),
        ),
        out_specs=P(pair_axes, None, band_axes),
        check_vma=False,
    )
```

time: 213 us -> 81.8 us (0.38)
  waiting for transfers between devices: 106 us -> 18.4 us
  Pallas kernels: 0 us -> 34.4 us
  local copies, waits for them, and re-layouts: 43.1 us -> 10.8 us
  matrix products: 26.3 us -> 0 us
  between operations: 13.3 us -> 0.09 us
  other arithmetic: 8.09 us -> 1.47 us
    reduce_scatter x2 -> x0, waiting for transfers between devices: 83.6 us -> none  [the longest x1 65 us: on_device(): lax.psum_scatter(spread, 'pair', scatter_dimension=0, tiled=True)]
    convert_element_type x3 -> x0, local copies, waits for them, and re-layouts: 34.7 us -> none  [on_device(): kernel = raw.reshape(NC, NC, NV, NV).transpose(2, 0, 3, 1).reshape(NV * N...]
    pallas_call x0 -> x4, Pallas kernels: none -> 34.4 us  [the longest x1 15.7 us: on_device(): call(apply_kernel, jax.ShapeDtypeStruct((2, count, NVC), BF16), [pltpu.VM...]
    dot_general x5 -> x0, matrix products: 26.3 us -> none  [the longest x2 21.7 us: transform(): lax.dot_general(basis_block, densities(first_set, second_set), (((1,), (0...]
    convert_element_type x5 -> x0, other arithmetic: 5.19 us -> none  [the longest x1 4.19 us: densities(): merged.reshape(first_set.shape[0], first_set.shape[1] * second_set.shape[1])]
    all_to_all x3, waiting for transfers between devices: 22.8 us -> 18.4 us  [the longest x1 9.89 us: on_device(): lax.all_to_all(out_send, all_axes, split_axis=0, concat_axis=0, tiled=True)]
    unnamed x12 -> x15, local copies, waits for them, and re-layouts: 1.03 us -> 5.1 us
    gather x4 -> x3, local copies, waits for them, and re-layouts: 5.64 us -> 3.47 us  [the longest x1 1.55 us: on_device(): trial_part = trial.transpose(1, 2, 0)[which]]
  transfers between devices with their start and end apart: 6 -> 4, of which waited for: 5 -> 2; matrix products, arithmetic and copies ran while one was open for 8% -> 5% of each run, Pallas kernels for 0% -> 21%
where the time goes in v1:
time: 81.8 us; the launch traced here: 81.3 us
  Pallas kernels  34.4 us (42%)
  waiting for transfers between devices  18.4 us (22%)
  starting transfers between devices  16.2 us (20%)
  local copies, waits for them, and re-layouts  10.8 us (13%)
  other arithmetic  1.47 us (2%)
    pallas_call x1, Pallas kernels, on_device(): call(apply_kernel, jax.ShapeDtypeStruct((2, count, NVC), BF16), [pltpu.VM...  15.7 us
    pallas_call x1, Pallas kernels, on_device(): call(transform_kernel, [jax.ShapeDtypeStruct((NVC, half), BF16)] * 3, [pl...  12.3 us
    all_to_all x1, waiting for transfers between devices, on_device(): lax.all_to_all(out_send, all_axes, split_axis=0, concat_axis=0, tiled=True)  9.89 us
    all_to_all x1, waiting for transfers between devices, on_device(): lax.all_to_all(send, pair_axes, split_axis=0, concat_axis=0, tiled=True)  8.5 us
    all_to_all x1, starting transfers between devices, on_device(): lax.all_to_all(send, pair_axes, split_axis=0, concat_axis=0, tiled=True)  7.31 us
    all_to_all x1, starting transfers between devices, on_device(): lax.all_to_all(out_send, all_axes, split_axis=0, concat_axis=0, tiled=True)  5.19 us
    unnamed x15, local copies, waits for them, and re-layouts  5.1 us
    pallas_call x1, Pallas kernels, on_device(): call(basis_kernel, jax.ShapeDtypeStruct((NR, 2 * half), BF16), [pltpu.VME...  4.7 us
  transfers between devices with their start and end apart: 4, of which 2 were waited for; matrix products, arithmetic and copies ran while one was open for 5% of the time, Pallas kernels for 21%

profile of v1, /device:TPU:0, one launch (start us, length us, event | category | flops | bytes accessed | tf_op | source)
XLA Modules:
  0.0 81.3 jit_solution(7013567437543510235)
XLA Ops:
  0.0 0.0 copy-start
  0.0 0.8 %reshape.73 = s32[4,2,2]{1,0,2:T(4,128)S(1)} reshape(s32[8,2]{0,1:T(2,128)} %param.8) | data formatting | bytes 128 | tf_op jit(solution)/shard_map/reshape | solution.py:258
  0.8 0.2 dynamic-slice_reduce_fusion
  1.1 0.1 copy.9
  1.2 0.1 reshape.80
  1.2 0.2 dynamic-slice_reduce_fusion.1
  1.5 0.0 copy-done
  1.5 0.6 gather_fusion
  2.1 1.6 %gather_fusion.1 = bf16[4,64,128]{2,1,0:T(8,128)(2,1)S(1)} fusion(bf16[23,64,128]{2,1,0:T(8,128)(2,1)} %bitcast.31, s32[1024]{0:T(1024)S(1)} %pad_clamp_fusion.1), kind=kCustom, calls=%fused_computation.1 | custom fusion | bytes 131088 | tf_op jit(solution)/shard_map/gather | solution.py:262
  3.6 0.8 maximum_maximum_fusion
  4.4 7.3 %all-to-all-start = ((bf16[8,64,384]{2,1,0:T(8,128)(2,1)}), bf16[8,64,384]{2,1,0:T(8,128)(2,1)S(1)}, u32[]{:S(2)}, u32[]{:S(2)}) async-start(bf16[8,64,384]{2,1,0:T(8,128)(2,1)} %maximum_maximum_fusion), calls=%async_computation | async-start | bytes 786432 | tf_op jit(solution)/shard_map/all_to_all | solution.py:265
  11.7 1.1 %copy.15 = bf16[128,8,256]{2,0,1:T(8,128)(2,1)S(1)} copy(bf16[128,8,256]{2,1,0:T(8,128)(2,1)} %param.6) | data formatting | bytes 1048576 | tf_op args[1]
  12.9 0.7 compare_select_fusion.1
  13.5 1.4 %gather_fusion.2 = bf16[8,128,256]{2,1,0:T(8,128)(2,1)} fusion(bf16[8,128,256]{2,1,0:T(8,128)(2,1)S(1)} %bitcast.26, s32[1024]{0:T(1024)S(1)} %pad_clamp_fusion), kind=kCustom, calls=%fused_computation.2 | custom fusion | bytes 1048608 | tf_op jit(solution)/shard_map/gather | solution.py:267
  14.9 8.5 %all-to-all-done.own_ref = bf16[8,64,384]{2,1,0:T(8,128)(2,1)S(1)} async-done(((bf16[8,64,384]{2,1,0:T(8,128)(2,1)}), bf16[8,64,384]{2,1,0:T(8,128)(2,1)S(1)}, u32[]{:S(2)}, u32[]{:S(2)}) %all-to-all-start) | async-done | bytes 393248 | tf_op jit(solution)/shard_map/all_to_all | solution.py:265
  23.4 3.7 %all-to-all-start.1 = ((bf16[8,128,256]{2,1,0:T(8,128)(2,1)}), bf16[8,128,256]{2,1,0:T(8,128)(2,1)S(1)}, u32[]{:S(2)}, u32[]{:S(2)}) async-start(bf16[8,128,256]{2,1,0:T(8,128)(2,1)} %gather_fusion.2), calls=%async_computation.1 | async-start | bytes 1048576 | tf_op jit(solution)/shard_map/all_to_all | solution.py:268
  27.1 0.0 collective-permute-start
  27.1 4.7 %basis.1.basis_ref = bf16[2048,1024]{1,0:T(8,128)(2,1)} custom-call(), custom_call_target="tpu_custom_call" | custom-call | flops 8388608 | bytes 4194304 | tf_op jit(solution)/shard_map/basis/pallas_call | solution.py:289
  31.8 0.0 collective-permute-done.other_ref
  31.8 0.0 copy-done.3
  31.8 0.8 copy-done.5
  32.6 12.3 %transform.1 = (bf16[1024,512]{1,0:T(8,128)(2,1)}, bf16[1024,512]{1,0:T(8,128)(2,1)}, bf16[1024,512]{1,0:T(8,128)(2,1)}) custom-call(bf16[8,64,384]{2,1,0:T(8,128)(2,1)} %copy-done.3, bf16[8,64,384]{2,1,0:T(8,128)(2,1)} %copy-done.5, bf16[2048,1024]{1,0:T(8,128)(2,1)} %basis.1.basis_ref), custom_call_target="tpu_custom_call" | custom-call | flops 4294967296 | bytes 4194304 | tf_op jit(solution)/shard_map/transform/pallas_call | solution.py:296
  44.8 0.0 all-to-all-done.1.screen_ref
  44.8 0.8 copy-done.2
  45.6 15.7 %apply.1 = bf16[2,64,1024]{2,1,0:T(8,128)(2,1)} custom-call(bf16[8,64,384]{2,1,0:T(8,128)(2,1)} %copy-done.3, bf16[8,64,384]{2,1,0:T(8,128)(2,1)} %copy-done.5, bf16[1024,512]{1,0:T(8,128)(2,1)} %get-tuple-element.8.val_ref, bf16[8,128,256]{2,1,0:T(8,128)(2,1)} %copy-done.2, bf16[1024,512]{1,0:T(8,128)(2,1)} %get-tuple-element.9.cond_ref, ...), custom_call_target="tpu_custom_call" | custom-call | flops 4831838208 | bytes 1048576 | tf_op jit(solution)/shard_map/apply/pallas_call | solution.py:309
  61.4 1.0 %copy.13 = bf16[16,8,8,128]{3,2,1,0:T(8,128)(2,1)S(1)} copy(bf16[16,8,8,128]{3,1,2,0:T(8,128)(2,1)} %bitcast.30) | data formatting | bytes 524288
  62.4 0.7 copy.11
  63.1 5.2 %all-to-all-start.2 = ((bf16[32,2,16,128]{3,2,1,0:T(8,128)(2,1)}), bf16[32,2,16,128]{3,2,1,0:T(8,128)(2,1)S(1)}, u32[]{:S(2)}, u32[]{:S(2)}) async-start(bf16[32,2,16,128]{3,2,1,0:T(8,128)(2,1)} %bitcast.6), calls=%async_computation.2 | async-start | bytes 524288 | tf_op jit(solution)/shard_map/all_to_all | solution.py:329
  68.3 0.7 copy.12.kpts_ref
  69.0 9.9 %all-to-all-done.2 = bf16[32,2,16,128]{3,2,1,0:T(8,128)(2,1)S(1)} async-done(((bf16[32,2,16,128]{3,2,1,0:T(8,128)(2,1)}), bf16[32,2,16,128]{3,2,1,0:T(8,128)(2,1)S(1)}, u32[]{:S(2)}, u32[]{:S(2)}) %all-to-all-start.2) | async-done | bytes 262176 | tf_op jit(solution)/shard_map/all_to_all | solution.py:329
  78.9 0.7 copy-done.1
  79.6 1.7 %gather.19 = f32[23,16,128]{2,1,0:T(8,128)} custom-call(s32[8,2]{1,0:T(8,128)} %copy.12.kpts_ref, bf16[2,4,2,2,2,16,128]{6,5,4,3,2,1,0:T(8,128)(2,1)} %bitcast.27), custom_call_target="tpu_custom_call" | custom-call | tf_op jit(solution)/shard_map/gather/pallas_call | solution.py:338
  (12 shorter events, 0.1 us)
Async XLA Ops:
  0.0 1.5 %copy-start = (bf16[256,23,64]{0,2,1:T(8,128)(2,1)S(1)}, bf16[256,23,64]{0,2,1:T(8,128)(2,1)}, u32[]{:S(2)}) copy-start(bf16[256,23,64]{0,2,1:T(8,128)(2,1)} %param.5) | copy-start | bytes 2260996
  4.4 19.0 %all-to-all-start = ((bf16[8,64,384]{2,1,0:T(8,128)(2,1)}), bf16[8,64,384]{2,1,0:T(8,128)(2,1)S(1)}, u32[]{:S(2)}, u32[]{:S(2)}) async-start(bf16[8,64,384]{2,1,0:T(8,128)(2,1)} %maximum_maximum_fusion), calls=%async_computation | async-start | bytes 786432 | tf_op jit(solution)/shard_map/all_to_all | solution.py:265
  23.4 8.4 %copy-start.3 = (bf16[8,64,384]{2,1,0:T(8,128)(2,1)}, bf16[8,64,384]{2,1,0:T(8,128)(2,1)S(1)}, u32[]{:S(2)}) copy-start(bf16[8,64,384]{2,1,0:T(8,128)(2,1)S(1)} %all-to-all-done.own_ref) | copy-start | bytes 1179652
  23.4 21.4 %all-to-all-start.1 = ((bf16[8,128,256]{2,1,0:T(8,128)(2,1)}), bf16[8,128,256]{2,1,0:T(8,128)(2,1)S(1)}, u32[]{:S(2)}, u32[]{:S(2)}) async-start(bf16[8,128,256]{2,1,0:T(8,128)(2,1)} %gather_fusion.2), calls=%async_computation.1 | async-start | bytes 1048576 | tf_op jit(solution)/shard_map/all_to_all | solution.py:268
  27.1 4.7 %collective-permute-start = (bf16[8,64,384]{2,1,0:T(8,128)(2,1)S(1)}, bf16[8,64,384]{2,1,0:T(8,128)(2,1)S(1)}, u32[]{:S(2)}, u32[]{:S(2)}) collective-permute-start(bf16[8,64,384]{2,1,0:T(8,128)(2,1)S(1)} %all-to-all-done.own_ref), channel_id=1, source_target_pairs={{0,1},{1,0},{2,3},{3,2},{4,5},{5,4},{6,7},{7,6},{8,9},{9,8},{10,11... | collective-permute-start | bytes 1179656 | tf_op jit(solution)/shard_map/ppermute | solution.py:270
  31.8 0.8 copy-start.5
  44.8 0.8 copy-start.2
  45.6 22.7 %copy-start.4 = (s32[8,2]{0,1:T(2,128)S(1)}, s32[8,2]{0,1:T(2,128)}, u32[]{:S(2)}) copy-start(s32[8,2]{0,1:T(2,128)} %param.8) | copy-start | bytes 196
  63.1 15.8 %all-to-all-start.2 = ((bf16[32,2,16,128]{3,2,1,0:T(8,128)(2,1)}), bf16[32,2,16,128]{3,2,1,0:T(8,128)(2,1)S(1)}, u32[]{:S(2)}, u32[]{:S(2)}) async-start(bf16[32,2,16,128]{3,2,1,0:T(8,128)(2,1)} %bitcast.6), calls=%async_computation.2 | async-start | bytes 524288 | tf_op jit(solution)/shard_map/all_to_all | solution.py:329
  78.9 0.7 copy-start.1

commit v2 on v1

v2 whole, which is shorter than its diff:
```python
import math

import jax
import jax.numpy as jnp
from jax import lax
from jax.experimental import pallas as pl
from jax.experimental.pallas import tpu as pltpu
from jax.sharding import Mesh, PartitionSpec as P

NV = 32
NC = 32
NR = 2048
NG = 1024
NVC = NV * NC
LANES = 128
HALVES = 2
TABLE = 64
F32 = jnp.float32
BF16 = jnp.bfloat16
VMEM_LIMIT = 36 * 1024 * 1024


def dot(a, b):
    return lax.dot_general(a, b, (((1,), (0,)), ((), ())), preferred_element_type=F32)


def dot_rows(a, b):
    return lax.dot_general(a, b, (((1,), (1,)), ((), ())), preferred_element_type=F32)


SPACES = {"s": pltpu.SMEM, "v": pltpu.VMEM, "h": pl.ANY}


def call(body, name, inputs, outputs, scratch=(), flops=0):
    specs, arrays = [], []
    for space, array in inputs:
        specs.append(pl.BlockSpec(memory_space=SPACES.get(space, pltpu.VMEM)))
        if space == "v":
            array = pltpu.with_memory_space_constraint(array, pltpu.VMEM)
        elif space == "h":
            array = pltpu.with_memory_space_constraint(array, pltpu.HBM)
        arrays.append(array)
    shapes, out_specs = [], []
    for space, shape, dtype in outputs:
        kind = {"v": pltpu.VMEM, "h": pltpu.HBM}.get(space, jax.ShapeDtypeStruct)
        shapes.append(kind(shape, dtype))
        out_specs.append(pl.BlockSpec(memory_space=SPACES.get(space, pltpu.VMEM)))
    return pl.pallas_call(
        body,
        out_shape=shapes,
        in_specs=specs,
        out_specs=out_specs,
        scratch_shapes=list(scratch),
        compiler_params=pltpu.CompilerParams(vmem_limit_bytes=VMEM_LIMIT),
        cost_estimate=pl.CostEstimate(flops=int(flops), transcendentals=0, bytes_accessed=1 << 20),
        name=name,
    )(*arrays)


def pack_kernel(kpts_ref, orbital_ref, trial_ref, out_ref, sems):
    bx, bc = lax.axis_index("bx"), lax.axis_index("bc")
    strips, low = lax.axis_size("bx"), lax.axis_size("pl")
    points = orbital_ref.shape[2]
    bands = pl.ds(pl.multiple_of(bc * NV, NV), NV)
    copies = []
    for d in range(out_ref.shape[0]):
        pair = d % low * strips + bx
        first, second, own = kpts_ref[0, pair], kpts_ref[1, pair], kpts_ref[bc, pair]
        for source, target in (
            (orbital_ref.at[first, bands, :], out_ref.at[d, pl.ds(0, NV), pl.ds(0, points)]),
            (orbital_ref.at[second, bands, :], out_ref.at[d, pl.ds(NV, NV), pl.ds(0, points)]),
            (trial_ref.at[own], out_ref.at[d, :, pl.ds(points, trial_ref.shape[2])]),
        ):
            copies.append(pltpu.make_async_copy(source, target, sems.at[len(copies)]))
    for copy in copies:
        copy.start()
    for copy in copies:
        copy.wait()


def make_basis(out_ref, cos_low, sin_low, cos_high, sin_high):
    columns = out_ref.shape[1]
    quarter = columns // 4
    groups = lax.axis_size("bc")
    strip = NG // (lax.axis_size("bx") * groups)
    column = lax.broadcasted_iota(jnp.int32, (1, columns), 1)
    odd = column // quarter % 2
    inner = column % quarter
    frequency = jnp.where(
        column < 2 * quarter,
        lax.axis_index("ph") * 2 * quarter + 2 * inner,
        (inner // (strip // 2) * groups + lax.axis_index("bc")) * strip + 2 * (inner % (strip // 2)),
    ) + odd
    period = 4 * NR
    unit = math.pi / (2 * NR)

    def angle(index):
        index = index & (period - 1)
        return jnp.where(index >= period // 2, index - period, index).astype(F32) * unit

    low = lax.broadcasted_iota(jnp.int32, (TABLE, columns), 0)
    low_angle = angle((2 * low + 1) * frequency)
    scale = math.sqrt(2.0 / NR)
    cos_low[...] = jnp.cos(low_angle) * scale
    sin_low[...] = jnp.sin(low_angle) * scale
    high = lax.broadcasted_iota(jnp.int32, cos_high.shape, 0)
    high_angle = angle(2 * TABLE * high * frequency)
    cos_high[...] = jnp.cos(high_angle)
    sin_high[...] = jnp.sin(high_angle)

    def step(block, carry):
        value = cos_low[...] * cos_high[pl.ds(block, 1), :] - sin_low[...] * sin_high[pl.ds(block, 1), :]
        out_ref[pl.ds(pl.multiple_of(block * TABLE, TABLE), TABLE), :] = value.astype(BF16)
        return carry

    lax.fori_loop(0, out_ref.shape[0] // TABLE, step, 0)


def prepare_kernel(q_ref, screen_ref, basis_ref, send_ref, cos_low, sin_low, cos_high, sin_high, ordered):
    make_basis(basis_ref, cos_low, sin_low, cos_high, sin_high)
    pairs, rows, columns = send_ref.shape
    kinds = screen_ref.shape[0] // rows
    source = lax.broadcasted_iota(jnp.int32, (columns, columns), 0)
    target = lax.broadcasted_iota(jnp.int32, (columns, columns), 1)
    wanted = target % (columns // 2) * 2 + target // (columns // 2)
    order = jnp.where(source == wanted, 1.0, 0.0).astype(BF16)
    result = dot(screen_ref[...], order)
    for t in range(columns // LANES):
        ordered[t] = result[:, t * LANES : (t + 1) * LANES]
    for p in range(pairs):
        q = q_ref[p]
        for odd in range(2):
            for t in range(columns // LANES):
                send_ref[p, odd * rows // 2 : (odd + 1) * rows // 2, t * LANES : (t + 1) * LANES] = ordered[
                    t, pl.ds(q + kinds * odd, rows // 2, stride=2 * kinds), :
                ].astype(BF16)


def transform_kernel(
    own_ref,
    other_ref,
    basis_ref,
    val_ref,
    cond_ref,
    swap_ref,
    diagonal_ref,
    first,
    second,
    even,
    odd,
    wide,
    vectors,
):
    side = lax.axis_index("bc")
    blocks, count, width = own_ref.shape
    points = NR // blocks
    states = NVC // blocks
    piece = 256 if points % 256 == 0 else LANES
    middle = NR // 2
    source = lax.broadcasted_iota(jnp.int32, (piece, piece), 0)
    target = lax.broadcasted_iota(jnp.int32, (piece, piece), 1)
    flip = jnp.where(source + target == piece - 1, 1.0, 0.0).astype(BF16)
    for slot, ref in ((side, own_ref), (1 - side, other_ref)):
        for start in range(0, middle, piece):
            ahead = ref[start // points, :, start % points : start % points + piece].astype(F32)
            mirror = NR - start - piece
            behind = dot(ref[mirror // points, :, mirror % points : mirror % points + piece], flip)
            for half, value in enumerate((ahead, behind)):
                first[slot, half, :, start : start + piece] = value[:NV]
                second[slot, half, :, start : start + piece] = value[NV:]
        for b in range(blocks):
            turned = ref[b, :, width - states :].astype(F32).T
            vectors[slot, b * states : (b + 1) * states, :] = jnp.concatenate([turned] * (LANES // count), axis=1)

    half = val_ref.shape[1]
    quarter = half // 2
    strips = lax.axis_size("bx")
    run = quarter // strips
    for kind in range(2):
        for v in range(NV):
            rows = slice(v * NV, (v + 1) * NV)
            ahead = first[kind, 0, v : v + 1, :] * second[kind, 0]
            behind = first[kind, 1, v : v + 1, :] * second[kind, 1]
            even[rows, :] = (ahead + behind).astype(BF16)
            odd[rows, :] = (ahead - behind).astype(BF16)
        for parity, density in enumerate((even, odd)):
            at = (2 * kind + parity) * quarter
            result = dot(density[...], basis_ref[:, at : at + quarter])
            if kind == 0:
                val_ref[:, parity * quarter : (parity + 1) * quarter] = result.astype(BF16)
            else:
                for s in range(strips):
                    part = result[:, s * run : (s + 1) * run]
                    to = (2 * s + parity) * run
                    cond_ref[:, to : to + run] = part.astype(BF16)
                    for t in range(run // LANES):
                        wide[to // LANES + t] = part[:, t * LANES : (t + 1) * LANES]
    swap_rows(wide, swap_ref)

    repeat = LANES // NV
    lanes = repeat * count
    lane = lax.broadcasted_iota(jnp.int32, (NV, lanes), 1) // count
    masks = [jnp.where(lane == r, 1.0, 0.0).astype(BF16) for r in range(repeat)]
    for kind in range(2):
        for d in range(NC):
            rows = vectors[1 - kind, pl.ds(d, NV, stride=NV), :].astype(BF16)
            rows = jnp.concatenate([rows] * (lanes // LANES), axis=1)
            for r in range(repeat):
                diagonal_ref[kind, d * LANES + r * NV : d * LANES + (r + 1) * NV, :] = rows * masks[r]


def swap_rows(wide, out_ref):
    for t in range(wide.shape[0]):
        for d in range(NC):
            out_ref[d * NC : (d + 1) * NC, t * LANES : (t + 1) * LANES] = wide[
                t, pl.ds(d, NC, stride=NC), :
            ].astype(BF16)


def apply_kernel(
    val_ref, screen_ref, cond_ref, swap_ref, diagonal_ref, out_ref, screen, wide, screened, slabs
):
    half = val_ref.shape[1]
    strips = lax.axis_size("bx")
    tall, broad = screen_ref.shape[1:]
    part = tall // 2
    for b in range(screen_ref.shape[0]):
        row, col = b // strips, b % strips
        for odd in range(2):
            at = odd * (half // 2) + row * part
            screen[at : at + part, col * broad : (col + 1) * broad] = screen_ref[b, odd * part : (odd + 1) * part]
    result = dot(val_ref[...], screen[...])
    for t in range(half // LANES):
        wide[t] = result[:, t * LANES : (t + 1) * LANES]
    screened[0] = result.astype(BF16)
    swap_rows(wide, screened.at[1])

    repeat = LANES // NV
    groups = NVC // LANES
    count = diagonal_ref.shape[2] // repeat
    scale = 1.0 / math.sqrt(NVC) / math.sqrt(NG)
    for kind in range(2):
        left_ref = swap_ref if kind == 0 else cond_ref
        raw = dot_rows(left_ref[...], screened[kind]).astype(BF16)
        for d in range(NC):
            for g in range(groups):
                slabs[kind, g * NC : (g + 1) * NC, d * LANES : (d + 1) * LANES] = raw[
                    d * NC : (d + 1) * NC, g * LANES : (g + 1) * LANES
                ]
        sides = dot(slabs[kind], diagonal_ref[kind]) * scale
        for g in range(groups):
            block = sides[g * NC : (g + 1) * NC, :]
            stacked = jnp.concatenate([block[:, r * count : (r + 1) * count] for r in range(repeat)], axis=0)
            turned = stacked.T.astype(BF16)
            if len(out_ref.shape) == 3:
                out_ref[kind, :, g * LANES : (g + 1) * LANES] = turned
            else:
                share, states = out_ref.shape[3:]
                i, at = g * LANES // states, g * LANES % states
                for b in range(out_ref.shape[1]):
                    out_ref[i, b, kind, :, at : at + LANES] = turned[b * share : (b + 1) * share]


def gather_kernel(kpts_ref, got_ref, out_ref):
    out_ref[...] = jnp.zeros_like(out_ref)
    halves, low, strips, groups = got_ref.shape[:4]
    for p in range(low * strips):
        for s in range(2):
            total = None
            for h in range(halves):
                for g in range(groups):
                    part = got_ref[h, p // strips, p % strips, g, s].astype(F32)
                    total = part if total is None else total + part
            k = kpts_ref[s, p]
            out_ref[k] += total


def table_scratch(columns, rows):
    return [pltpu.VMEM((TABLE, columns), F32)] * 2 + [pltpu.VMEM((rows // TABLE, columns), F32)] * 2


def on_device(orbitals, screening, trial, pair_kpts, pair_q):
    halves, low, strips, groups = (lax.axis_size(a) for a in ("ph", "pl", "bx", "bc"))
    pair_axes, all_axes = ("ph", "pl"), ("ph", "pl", "bx", "bc")
    pair_count = halves * low
    points, kpt_count, _ = orbitals.shape
    states, _, count = trial.shape
    tall, kinds, broad = screening.shape
    half = NG // HALVES
    aligned = points % LANES == 0 and states % LANES == 0
    orbital_t, trial_t = orbitals.transpose(1, 2, 0), trial.transpose(1, 2, 0)
    kpts_t = pair_kpts.T
    basis_out = ("v", (NR // 2, 2 * half), BF16)

    if aligned:
        send = call(
            pack_kernel,
            "pack",
            [("s", kpts_t), ("h", orbital_t), ("h", trial_t)],
            [("h", (pair_count, count, points + states), BF16)],
            [pltpu.SemaphoreType.DMA((3 * pair_count,))],
        )[0]
        basis, screen_send = call(
            prepare_kernel,
            "prepare",
            [("s", pair_q), ("b", screening.reshape(tall * kinds, broad))],
            [basis_out, ("h" if False else "b", (low * strips, tall, broad), BF16)],
            table_scratch(2 * half, NR // 2) + [pltpu.VMEM((broad // LANES, tall * kinds, LANES), F32)],
            flops=NR * NG * 4,
        )
    else:
        bx, bc = lax.axis_index("bx"), lax.axis_index("bc")
        near = lax.dynamic_index_in_dim(pair_kpts.reshape(low, strips, 2), bx, 1, keepdims=False)
        orbital_half = lax.dynamic_slice_in_dim(orbital_t, bc * NV, NV, 1)
        orbital_part = orbital_half[near].reshape(low, 2 * NV, points)
        trial_part = trial_t[lax.dynamic_index_in_dim(near, bc, 1, keepdims=False)]
        send = jnp.concatenate([orbital_part, trial_part], axis=2)
        send = jnp.concatenate([send] * halves, axis=0)
        basis = call(make_basis, "basis", [], [basis_out], table_scratch(2 * half, NR // 2), flops=NR * NG)[0]
        screen_send = screening.transpose(1, 0, 2)[pair_q]
    got = lax.all_to_all(send, pair_axes, split_axis=0, concat_axis=0, tiled=True)
    screen_got = lax.all_to_all(screen_send, ("pl", "bx"), split_axis=0, concat_axis=0, tiled=True)
    other = lax.ppermute(got, "bc", [(i, i ^ 1) for i in range(groups)])

    if not aligned:

        def joined(x):
            turned = x.transpose(1, 0, 2)
            return jnp.concatenate(
                [turned[:, :, :points].reshape(1, count, NR), turned[:, :, points:].reshape(1, count, NVC)], axis=2
            )

        got, other = joined(got), joined(other)
        screen_got = screen_got.reshape(low, strips, tall // 2, 2, broad // 2, 2).transpose(1, 3, 0, 2, 5, 4)
        screen_got = screen_got.reshape(strips, low * tall, broad)

    valence, conduction, swapped, diagonal = call(
        transform_kernel,
        "transform",
        [("v", got), ("v", other), ("v", basis)],
        [("v", (NVC, half), BF16)] * 3 + [("v", (2, NC * LANES, LANES // NV * count), BF16)],
        [
            pltpu.VMEM((2, 2, NV, NR // 2), F32),
            pltpu.VMEM((2, 2, NV, NR // 2), F32),
            pltpu.VMEM((NVC, NR // 2), BF16),
            pltpu.VMEM((NVC, NR // 2), BF16),
            pltpu.VMEM((half // LANES, NVC, LANES), F32),
            pltpu.VMEM((2, NVC, LANES), F32),
        ],
        flops=2 * NVC * NR * half,
    )
    share = count // (strips * groups)
    partial = call(
        apply_kernel,
        "apply",
        [("v", valence), ("v", screen_got), ("v", conduction), ("v", swapped), ("v", diagonal)],
        [("b", (pair_count, strips * groups, 2, share, states) if aligned else (2, count, NVC), BF16)],
        [
            pltpu.VMEM((half, half), BF16),
            pltpu.VMEM((half // LANES, NVC, LANES), F32),
            pltpu.VMEM((2, NVC, half), BF16),
            pltpu.VMEM((2, NVC // LANES * NC, NC * LANES), BF16),
        ],
        flops=2 * NVC * half * half + 8 * NVC * NVC * half,
    )[0]
    if not aligned:
        partial = partial.reshape(2, strips * groups, share, pair_count, states).transpose(3, 1, 0, 2, 4)
    out_send = partial.reshape(pair_count * strips * groups, 2, share, states)
    out_got = lax.all_to_all(out_send, all_axes, split_axis=0, concat_axis=0, tiled=True)
    out_got = out_got.reshape(halves, low, strips, groups, 2, share, states)
    if aligned:
        applied = call(
            gather_kernel,
            "gather",
            [("s", kpts_t), ("v", out_got)],
            [("b", (kpt_count, share, states), F32)],
        )[0]
    else:
        summed = jnp.sum(out_got.astype(F32), axis=(0, 3)).reshape(-1, share * states)
        hot = (pair_kpts.reshape(-1)[None, :] == jnp.arange(kpt_count)[:, None]).astype(F32)
        applied = lax.dot_general(
            hot, summed, (((1,), (0,)), ((), ())), precision=lax.Precision.HIGHEST, preferred_element_type=F32
        ).reshape(kpt_count, share, states)
    return applied.transpose(2, 0, 1)


def solution(mesh):
    pair_count, band_count = mesh.shape["pair"], mesh.shape["band"]
    shape = (HALVES, pair_count // HALVES, 2, band_count // 2)
    fine = Mesh(mesh.devices.reshape(shape), ("ph", "pl", "bx", "bc"))
    pair_axes, band_axes = ("ph", "pl"), ("bx", "bc")
    return jax.shard_map(
        on_device,
        mesh=fine,
        in_specs=(
            P(pair_axes, None, None),
            P(pair_axes, None, band_axes),
            P(pair_axes, None, None),
            P(),
            P(),
        ),
        out_specs=P(pair_axes, None, band_axes),
        check_vma=False,
    )
```

time: 81.8 us -> 79.1 us (0.967)
  blocking collectives: 0 us -> 15.4 us
  waiting for transfers between devices: 18.4 us -> 7.75 us
  starting transfers between devices: 16.2 us -> 11.1 us
  Pallas kernels: 34.4 us -> 31.1 us
  local copies, waits for them, and re-layouts: 10.8 us -> 13.2 us
  other arithmetic: 1.47 us -> 0 us
    all_to_all x0 -> x1, blocking collectives: none -> 15.4 us  [on_device(): lax.all_to_all(out_send, all_axes, split_axis=0, concat_axis=0, tiled=True)]
    all_to_all x1 -> x0, waiting for transfers between devices: 9.89 us -> none  [on_device(): lax.all_to_all(out_send, all_axes, split_axis=0, concat_axis=0, tiled=True)]
    unnamed x15 -> x24, local copies, waits for them, and re-layouts: 5.1 us -> 13.2 us
    all_to_all x1 -> x0, starting transfers between devices: 5.19 us -> none  [on_device(): lax.all_to_all(out_send, all_axes, split_axis=0, concat_axis=0, tiled=True)]
    gather x3 -> x0, local copies, waits for them, and re-layouts: 3.47 us -> none  [the longest x1 1.55 us: on_device(): trial_part = trial.transpose(1, 2, 0)[which]]
    pallas_call x4 -> x5, Pallas kernels: 34.4 us -> 31.1 us  [call(): pl.pallas_call(body, out_shape=shapes, in_specs=specs, out_specs=out_spec...]
    all_to_all x1, waiting for transfers between devices: 8.5 us -> 6.04 us  [on_device(): lax.all_to_all(send, pair_axes, split_axis=0, concat_axis=0, tiled=True)]
    ppermute x1, waiting for transfers between devices: 0.01 us -> 1.71 us  [on_device(): other = lax.ppermute(got, 'bc', [(i, i ^ 1) for i in range(groups)])]
  transfers between devices with their start and end apart: 4 -> 3, of which waited for: 2 -> 2; matrix products, arithmetic and copies ran while one was open for 5% -> 0% of each run, Pallas kernels for 21% -> 12%
where the time goes in v2:
time: 79.1 us; the launch traced here: 78.5 us
  Pallas kernels  31.1 us (39%)
  blocking collectives  15.4 us (19%)
  local copies, waits for them, and re-layouts  13.2 us (17%)
  starting transfers between devices  11.1 us (14%)
  waiting for transfers between devices  7.75 us (10%)
    pallas_call x5, Pallas kernels, call(): pl.pallas_call(body, out_shape=shapes, in_specs=specs, out_specs=out_spec...  31.1 us
    all_to_all x1, blocking collectives, on_device(): lax.all_to_all(out_send, all_axes, split_axis=0, concat_axis=0, tiled=True)  15.4 us
    unnamed x24, local copies, waits for them, and re-layouts  13.2 us
    all_to_all x1, starting transfers between devices, on_device(): lax.all_to_all(send, pair_axes, split_axis=0, concat_axis=0, tiled=True)  7.32 us
    all_to_all x1, waiting for transfers between devices, on_device(): lax.all_to_all(send, pair_axes, split_axis=0, concat_axis=0, tiled=True)  6.04 us
    all_to_all x1, starting transfers between devices, on_device(): lax.all_to_all(screen_send, ('pl', 'bx'), split_axis=0, concat_axis=0, ti...  3.67 us
    ppermute x1, waiting for transfers between devices, on_device(): other = lax.ppermute(got, 'bc', [(i, i ^ 1) for i in range(groups)])  1.71 us
  transfers between devices with their start and end apart: 3, of which 2 were waited for; matrix products, arithmetic and copies ran while one was open for 0% of the time, Pallas kernels for 12%

profile of v2, /device:TPU:0, one launch (start us, length us, event | category | flops | bytes accessed | tf_op | source)
XLA Modules:
  0.0 78.5 jit_solution(16915720879649832974)
XLA Ops:
  0.0 0.0 copy-start.1
  0.0 0.7 copy-done.1
  0.7 13.8 %pack.1 = bf16[8,64,384]{2,1,0:T(8,128)(2,1)} custom-call(s32[2,8]{1,0:T(2,128)S(1)} %bitcast.10, bf16[23,64,256]{2,1,0:T(8,128)(2,1)} %bitcast.12, bf16[23,64,128]{2,1,0:T(8,128)(2,1)} %bitcast.13), custom_call_target="tpu_custom_call" | custom-call | bytes 1048576 | tf_op jit(solution)/shard_map/pack/pallas_call | solution.py:48
  14.5 7.3 %all-to-all-start = ((bf16[8,64,384]{2,1,0:T(8,128)(2,1)}), bf16[8,64,384]{2,1,0:T(8,128)(2,1)S(1)}, u32[]{:S(2)}, u32[]{:S(2)}) async-start(bf16[8,64,384]{2,1,0:T(8,128)(2,1)} %pack.1), calls=%async_computation | async-start | bytes 786432 | tf_op jit(solution)/shard_map/all_to_all | solution.py:321
  21.8 0.0 copy-start
  21.8 1.0 %copy-done = bf16[128,8,256]{2,1,0:T(8,128)(2,1)S(1)} copy-done((bf16[128,8,256]{2,1,0:T(8,128)(2,1)S(1)}, bf16[128,8,256]{2,1,0:T(8,128)(2,1)}, u32[]{:S(2)}) %copy-start) | copy-done | bytes 524312
  22.9 0.0 copy-start.3
  22.9 0.7 copy-done.3
  23.5 3.9 %prepare.1 = (bf16[1024,1024]{1,0:T(8,128)(2,1)S(1)}, bf16[8,128,256]{2,1,0:T(8,128)(2,1)}) custom-call(s32[8]{0:T(128)S(1)} %copy-done.3, bf16[1024,256]{1,0:T(8,128)(2,1)S(1)} %bitcast.8), custom_call_target="tpu_custom_call" | custom-call | flops 8388608 | bytes 1048576 | tf_op jit(solution)/shard_map/prepare/pallas_call | solution.py:48
  27.4 6.0 %all-to-all-done.own_ref = bf16[8,64,384]{2,1,0:T(8,128)(2,1)S(1)} async-done(((bf16[8,64,384]{2,1,0:T(8,128)(2,1)}), bf16[8,64,384]{2,1,0:T(8,128)(2,1)S(1)}, u32[]{:S(2)}, u32[]{:S(2)}) %all-to-all-start) | async-done | bytes 393248 | tf_op jit(solution)/shard_map/all_to_all | solution.py:321
  33.5 3.7 %all-to-all-start.1 = ((bf16[8,128,256]{2,1,0:T(8,128)(2,1)}), bf16[8,128,256]{2,1,0:T(8,128)(2,1)S(1)}, u32[]{:S(2)}, u32[]{:S(2)}) async-start(bf16[8,128,256]{2,1,0:T(8,128)(2,1)} %get-tuple-element.13), calls=%async_computation.1 | async-start | bytes 1048576 | tf_op jit(solution)/shard_map/all_to_all | solution.py:322
  37.2 0.1 collective-permute-start
  37.2 1.7 %collective-permute-done.other_ref = bf16[8,64,384]{2,1,0:T(8,128)(2,1)S(1)} collective-permute-done((bf16[8,64,384]{2,1,0:T(8,128)(2,1)S(1)}, bf16[8,64,384]{2,1,0:T(8,128)(2,1)S(1)}, u32[]{:S(2)}, u32[]{:S(2)}) %collective-permute-start) | collective-permute-done | bytes 393248 | tf_op jit(solution)/shard_map/ppermute | solution.py:323
  39.0 5.6 %transform.1 = (bf16[1024,512]{1,0:T(8,128)(2,1)S(1)}, bf16[1024,512]{1,0:T(8,128)(2,1)S(1)}, bf16[1024,512]{1,0:T(8,128)(2,1)S(1)}, bf16[2,4096,256]{2,1,0:T(8,128)(2,1)S(1)}) custom-call(bf16[8,64,384]{2,1,0:T(8,128)(2,1)S(1)} %all-to-all-done.own_ref, bf16[8,64,384]{2,1,0:T(8,128)(2,1)S(1)} %collective-permute-done.other_ref, ...), custom_call_target="tpu_custom_call" | custom-call | flops 2147483648 | bytes 1048576 | tf_op jit(solution)/shard_map/transform/pallas_call | solution.py:48
  44.6 0.0 copy-start.4
  44.6 1.9 %copy-done.4 = bf16[2,4096,256]{2,1,0:T(8,128)(2,1)} copy-done((bf16[2,4096,256]{2,1,0:T(8,128)(2,1)}, bf16[2,4096,256]{2,1,0:T(8,128)(2,1)S(1)}, u32[]{:S(2)}) %copy-start.4) | copy-done | bytes 4194328
  46.6 0.0 copy-start.6
  46.6 1.0 %copy-done.6 = bf16[1024,512]{1,0:T(8,128)(2,1)} copy-done((bf16[1024,512]{1,0:T(8,128)(2,1)}, bf16[1024,512]{1,0:T(8,128)(2,1)S(1)}, u32[]{:S(2)}) %copy-start.6) | copy-done | bytes 1048600
  47.5 0.0 copy-start.8
  47.5 1.0 %copy-done.8 = bf16[1024,512]{1,0:T(8,128)(2,1)} copy-done((bf16[1024,512]{1,0:T(8,128)(2,1)}, bf16[1024,512]{1,0:T(8,128)(2,1)S(1)}, u32[]{:S(2)}) %copy-start.8) | copy-done | bytes 1048600
  48.6 0.0 copy-start.10
  48.6 1.0 %copy-done.10 = bf16[1024,512]{1,0:T(8,128)(2,1)} copy-done((bf16[1024,512]{1,0:T(8,128)(2,1)}, bf16[1024,512]{1,0:T(8,128)(2,1)S(1)}, u32[]{:S(2)}) %copy-start.10) | copy-done | bytes 1048600
  49.5 0.0 all-to-all-done.1.screen_ref
  49.5 2.2 %copy-done.5 = bf16[2,4096,256]{2,1,0:T(8,128)(2,1)S(1)} copy-done((bf16[2,4096,256]{2,1,0:T(8,128)(2,1)S(1)}, bf16[2,4096,256]{2,1,0:T(8,128)(2,1)}, u32[]{:S(2)}) %copy-start.5) | copy-done | bytes 4194328
  51.7 0.0 copy-start.7
  51.7 1.2 %copy-done.7 = bf16[1024,512]{1,0:T(8,128)(2,1)S(1)} copy-done((bf16[1024,512]{1,0:T(8,128)(2,1)S(1)}, bf16[1024,512]{1,0:T(8,128)(2,1)}, u32[]{:S(2)}) %copy-start.7) | copy-done | bytes 1048600
  53.0 1.2 %copy-done.9 = bf16[1024,512]{1,0:T(8,128)(2,1)S(1)} copy-done((bf16[1024,512]{1,0:T(8,128)(2,1)S(1)}, bf16[1024,512]{1,0:T(8,128)(2,1)}, u32[]{:S(2)}) %copy-start.9) | copy-done | bytes 1048600
  54.2 1.2 %copy-done.11 = bf16[1024,512]{1,0:T(8,128)(2,1)S(1)} copy-done((bf16[1024,512]{1,0:T(8,128)(2,1)S(1)}, bf16[1024,512]{1,0:T(8,128)(2,1)}, u32[]{:S(2)}) %copy-start.11) | copy-done | bytes 1048600
  55.4 6.4 %apply.1 = bf16[8,4,2,16,128]{4,3,2,1,0:T(8,128)(2,1)S(1)} custom-call(bf16[1024,512]{1,0:T(8,128)(2,1)S(1)} %copy-done.7, bf16[8,128,256]{2,1,0:T(8,128)(2,1)S(1)} %all-to-all-done.1.screen_ref, bf16[1024,512]{1,0:T(8,128)(2,1)S(1)} %copy-done.9, bf16[1024,512]{1,0:T(8,128)(2,1)S(1)} %copy-done.11, bf16[2,4096,256]{2,1,0:T(8,128)(2,1)S(1)} %copy-done.5), custom_call_target="tpu_custom_call" | custom-call | flops 4831838208 | bytes 1048576 | tf_op jit(solution)/shard_map/apply/pallas_call | solution.py:48
  61.8 15.4 %all_to_all.15 = bf16[32,2,16,128]{3,2,1,0:T(8,128)(2,1)S(1)} all-to-all(bf16[32,2,16,128]{3,2,1,0:T(8,128)(2,1)S(1)} %bitcast.9), channel_id=1, replica_groups=mesh['ph'=2,'pl'=4,'bx'=2,'bc'=2] {'ph','pl','bx','bc'}, dimensions={0} | all-to-all | bytes 524288 | tf_op jit(solution)/shard_map/all_to_all | solution.py:369
  77.2 0.0 copy-done.2
  77.2 1.3 %gather.1 = f32[23,16,128]{2,1,0:T(8,128)} custom-call(s32[2,8]{1,0:T(2,128)S(1)} %bitcast.11, bf16[2,4,2,2,2,16,128]{6,5,4,3,2,1,0:T(8,128)(2,1)S(1)} %bitcast.7), custom_call_target="tpu_custom_call" | custom-call | bytes 1048576 | tf_op jit(solution)/shard_map/gather/pallas_call | solution.py:48
  (4 shorter events, 0.0 us)
Async XLA Ops:
  0.0 0.7 copy-start.1
  14.5 19.0 %all-to-all-start = ((bf16[8,64,384]{2,1,0:T(8,128)(2,1)}), bf16[8,64,384]{2,1,0:T(8,128)(2,1)S(1)}, u32[]{:S(2)}, u32[]{:S(2)}) async-start(bf16[8,64,384]{2,1,0:T(8,128)(2,1)} %pack.1), calls=%async_computation | async-start | bytes 786432 | tf_op jit(solution)/shard_map/all_to_all | solution.py:321
  21.8 1.0 %copy-start = (bf16[128,8,256]{2,1,0:T(8,128)(2,1)S(1)}, bf16[128,8,256]{2,1,0:T(8,128)(2,1)}, u32[]{:S(2)}) copy-start(bf16[128,8,256]{2,1,0:T(8,128)(2,1)} %param.6) | copy-start | bytes 1572868
  22.9 0.7 copy-start.3
  33.5 16.1 %all-to-all-start.1 = ((bf16[8,128,256]{2,1,0:T(8,128)(2,1)}), bf16[8,128,256]{2,1,0:T(8,128)(2,1)S(1)}, u32[]{:S(2)}, u32[]{:S(2)}) async-start(bf16[8,128,256]{2,1,0:T(8,128)(2,1)} %get-tuple-element.13), calls=%async_computation.1 | async-start | bytes 1048576 | tf_op jit(solution)/shard_map/all_to_all | solution.py:322
  37.2 1.8 %collective-permute-start = (bf16[8,64,384]{2,1,0:T(8,128)(2,1)S(1)}, bf16[8,64,384]{2,1,0:T(8,128)(2,1)S(1)}, u32[]{:S(2)}, u32[]{:S(2)}) collective-permute-start(bf16[8,64,384]{2,1,0:T(8,128)(2,1)S(1)} %all-to-all-done.own_ref), channel_id=1, source_target_pairs={{0,1},{1,0},{2,3},{3,2},{4,5},{5,4},{6,7},{7,6},{8,9},{9,8},{10,11... | collective-permute-start | bytes 1179656 | tf_op jit(solution)/shard_map/ppermute | solution.py:323
  44.6 2.0 %copy-start.4 = (bf16[2,4096,256]{2,1,0:T(8,128)(2,1)}, bf16[2,4096,256]{2,1,0:T(8,128)(2,1)S(1)}, u32[]{:S(2)}) copy-start(bf16[2,4096,256]{2,1,0:T(8,128)(2,1)S(1)} %get-tuple-element.16.diagonal_ref) | copy-start | bytes 12582916
  46.6 1.0 %copy-start.6 = (bf16[1024,512]{1,0:T(8,128)(2,1)}, bf16[1024,512]{1,0:T(8,128)(2,1)S(1)}, u32[]{:S(2)}) copy-start(bf16[1024,512]{1,0:T(8,128)(2,1)S(1)} %get-tuple-element.12.val_ref) | copy-start | bytes 3145732
  47.5 1.0 %copy-start.8 = (bf16[1024,512]{1,0:T(8,128)(2,1)}, bf16[1024,512]{1,0:T(8,128)(2,1)S(1)}, u32[]{:S(2)}) copy-start(bf16[1024,512]{1,0:T(8,128)(2,1)S(1)} %get-tuple-element.14.cond_ref) | copy-start | bytes 3145732
  48.6 1.0 %copy-start.10 = (bf16[1024,512]{1,0:T(8,128)(2,1)}, bf16[1024,512]{1,0:T(8,128)(2,1)S(1)}, u32[]{:S(2)}) copy-start(bf16[1024,512]{1,0:T(8,128)(2,1)S(1)} %get-tuple-element.15.swap_ref) | copy-start | bytes 3145732
  49.5 2.2 %copy-start.5 = (bf16[2,4096,256]{2,1,0:T(8,128)(2,1)S(1)}, bf16[2,4096,256]{2,1,0:T(8,128)(2,1)}, u32[]{:S(2)}) copy-start(bf16[2,4096,256]{2,1,0:T(8,128)(2,1)} %copy-done.4) | copy-start | bytes 12582916
  51.7 1.2 %copy-start.7 = (bf16[1024,512]{1,0:T(8,128)(2,1)S(1)}, bf16[1024,512]{1,0:T(8,128)(2,1)}, u32[]{:S(2)}) copy-start(bf16[1024,512]{1,0:T(8,128)(2,1)} %copy-done.6) | copy-start | bytes 3145732
  53.0 1.2 %copy-start.9 = (bf16[1024,512]{1,0:T(8,128)(2,1)S(1)}, bf16[1024,512]{1,0:T(8,128)(2,1)}, u32[]{:S(2)}) copy-start(bf16[1024,512]{1,0:T(8,128)(2,1)} %copy-done.8) | copy-start | bytes 3145732
  54.2 1.2 %copy-start.11 = (bf16[1024,512]{1,0:T(8,128)(2,1)S(1)}, bf16[1024,512]{1,0:T(8,128)(2,1)}, u32[]{:S(2)}) copy-start(bf16[1024,512]{1,0:T(8,128)(2,1)} %copy-done.10) | copy-start | bytes 3145732
  55.4 21.8 %copy-start.2 = (s32[8,2]{0,1:T(2,128)S(1)}, s32[8,2]{0,1:T(2,128)}, u32[]{:S(2)}) copy-start(s32[8,2]{0,1:T(2,128)} %param.8) | copy-start | bytes 196

commit v3 on v2

--- a/solution.py
+++ b/solution.py
@@ -35,10 +35,8 @@
     specs, arrays = [], []
     for space, array in inputs:
         specs.append(pl.BlockSpec(memory_space=SPACES.get(space, pltpu.VMEM)))
-        if space == "v":
-            array = pltpu.with_memory_space_constraint(array, pltpu.VMEM)
-        elif space == "h":
-            array = pltpu.with_memory_space_constraint(array, pltpu.HBM)
+        home = pltpu.VMEM if space == "v" else pltpu.HBM
+        array = pltpu.with_memory_space_constraint(array, home)
         arrays.append(array)
     shapes, out_specs = [], []
     for space, shape, dtype in outputs:
@@ -150,6 +148,11 @@
     odd,
     wide,
     vectors,
+    valence,
+    conduction,
+    swapped,
+    diagonal,
+    sems,
 ):
     side = lax.axis_index("bc")
     blocks, count, width = own_ref.shape
@@ -172,11 +175,30 @@
             turned = ref[b, :, width - states :].astype(F32).T
             vectors[slot, b * states : (b + 1) * states, :] = jnp.concatenate([turned] * (LANES // count), axis=1)
 
+    copies = []
+    repeat = LANES // NV
+    lanes = repeat * count
+    lane = lax.broadcasted_iota(jnp.int32, (NV, lanes), 1) // count
+    masks = [jnp.where(lane == r, 1.0, 0.0).astype(BF16) for r in range(repeat)]
+    for kind in range(2):
+        for d in range(NC):
+            rows = vectors[1 - kind, pl.ds(d, NV, stride=NV), :].astype(BF16)
+            rows = jnp.concatenate([rows] * (lanes // LANES), axis=1)
+            for r in range(repeat):
+                diagonal[kind, d * LANES + r * NV : d * LANES + (r + 1) * NV, :] = rows * masks[r]
+
+        copies.append(pltpu.make_async_copy(diagonal.at[kind], diagonal_ref.at[kind], sems.at[kind]))
+        copies[-1].start()
     half = val_ref.shape[1]
     quarter = half // 2
     strips = lax.axis_size("bx")
     run = quarter // strips
-    for kind in range(2):
+
+    def flush(source, target):
+        copies.append(pltpu.make_async_copy(source, target, sems.at[len(copies)]))
+        copies[-1].start()
+
+    for kind in (1, 0):
         for v in range(NV):
             rows = slice(v * NV, (v + 1) * NV)
             ahead = first[kind, 0, v : v + 1, :] * second[kind, 0]
@@ -187,26 +209,21 @@
             at = (2 * kind + parity) * quarter
             result = dot(density[...], basis_ref[:, at : at + quarter])
             if kind == 0:
-                val_ref[:, parity * quarter : (parity + 1) * quarter] = result.astype(BF16)
+                valence[:, parity * quarter : (parity + 1) * quarter] = result.astype(BF16)
             else:
                 for s in range(strips):
                     part = result[:, s * run : (s + 1) * run]
                     to = (2 * s + parity) * run
-                    cond_ref[:, to : to + run] = part.astype(BF16)
+                    conduction[:, to : to + run] = part.astype(BF16)
                     for t in range(run // LANES):
                         wide[to // LANES + t] = part[:, t * LANES : (t + 1) * LANES]
-    swap_rows(wide, swap_ref)
-
-    repeat = LANES // NV
-    lanes = repeat * count
-    lane = lax.broadcasted_iota(jnp.int32, (NV, lanes), 1) // count
-    masks = [jnp.where(lane == r, 1.0, 0.0).astype(BF16) for r in range(repeat)]
-    for kind in range(2):
-        for d in range(NC):
-            rows = vectors[1 - kind, pl.ds(d, NV, stride=NV), :].astype(BF16)
-            rows = jnp.concatenate([rows] * (lanes // LANES), axis=1)
-            for r in range(repeat):
-                diagonal_ref[kind, d * LANES + r * NV : d * LANES + (r + 1) * NV, :] = rows * masks[r]
+        if kind == 1:
+            flush(conduction, cond_ref)
+            swap_rows(wide, swapped)
+            flush(swapped, swap_ref)
+    flush(valence, val_ref)
+    for copy in copies:
+        copy.wait()
 
 
 def swap_rows(wide, out_ref):
@@ -218,8 +235,27 @@
 
 
 def apply_kernel(
-    val_ref, screen_ref, cond_ref, swap_ref, diagonal_ref, out_ref, screen, wide, screened, slabs
+    val_ref,
+    screen_ref,
+    cond_ref,
+    swap_ref,
+    diagonal_ref,
+    out_ref,
+    screen,
+    wide,
+    screened,
+    slabs,
+    valence,
+    conduction,
+    swapped,
+    diagonal,
+    sems,
 ):
+    sources = (diagonal_ref.at[0], diagonal_ref.at[1], swap_ref, cond_ref, val_ref)
+    targets = (diagonal.at[0], diagonal.at[1], swapped, conduction, valence)
+    copies = [pltpu.make_async_copy(a, b, sems.at[i]) for i, (a, b) in enumerate(zip(sources, targets))]
+    for k in (4, 3, 1, 2, 0):
+        copies[k].start()
     half = val_ref.shape[1]
     strips = lax.axis_size("bx")
     tall, broad = screen_ref.shape[1:]
@@ -229,7 +265,8 @@
         for odd in range(2):
             at = odd * (half // 2) + row * part
             screen[at : at + part, col * broad : (col + 1) * broad] = screen_ref[b, odd * part : (odd + 1) * part]
-    result = dot(val_ref[...], screen[...])
+    copies[4].wait()
+    result = dot(valence[...], screen[...])
     for t in range(half // LANES):
         wide[t] = result[:, t * LANES : (t + 1) * LANES]
     screened[0] = result.astype(BF16)
@@ -239,15 +276,17 @@
     groups = NVC // LANES
     count = diagonal_ref.shape[2] // repeat
     scale = 1.0 / math.sqrt(NVC) / math.sqrt(NG)
-    for kind in range(2):
-        left_ref = swap_ref if kind == 0 else cond_ref
+    for kind in (1, 0):
+        left_ref = swapped if kind == 0 else conduction
+        copies[2 + kind].wait()
         raw = dot_rows(left_ref[...], screened[kind]).astype(BF16)
         for d in range(NC):
             for g in range(groups):
                 slabs[kind, g * NC : (g + 1) * NC, d * LANES : (d + 1) * LANES] = raw[
                     d * NC : (d + 1) * NC, g * LANES : (g + 1) * LANES
                 ]
-        sides = dot(slabs[kind], diagonal_ref[kind]) * scale
+        copies[kind].wait()
+        sides = dot(slabs[kind], diagonal[kind]) * scale
         for g in range(groups):
             block = sides[g * NC : (g + 1) * NC, :]
             stacked = jnp.concatenate([block[:, r * count : (r + 1) * count] for r in range(repeat)], axis=0)
@@ -297,14 +336,14 @@
             pack_kernel,
             "pack",
             [("s", kpts_t), ("h", orbital_t), ("h", trial_t)],
-            [("h", (pair_count, count, points + states), BF16)],
+            [("v", (pair_count, count, points + states), BF16)],
             [pltpu.SemaphoreType.DMA((3 * pair_count,))],
         )[0]
         basis, screen_send = call(
             prepare_kernel,
             "prepare",
             [("s", pair_q), ("b", screening.reshape(tall * kinds, broad))],
-            [basis_out, ("h" if False else "b", (low * strips, tall, broad), BF16)],
+            [basis_out, ("v", (low * strips, tall, broad), BF16)],
             table_scratch(2 * half, NR // 2) + [pltpu.VMEM((broad // LANES, tall * kinds, LANES), F32)],
             flops=NR * NG * 4,
         )
@@ -334,11 +373,12 @@
         screen_got = screen_got.reshape(low, strips, tall // 2, 2, broad // 2, 2).transpose(1, 3, 0, 2, 5, 4)
         screen_got = screen_got.reshape(strips, low * tall, broad)
 
+    diagonals = (2, NC * LANES, LANES // NV * count)
     valence, conduction, swapped, diagonal = call(
         transform_kernel,
         "transform",
         [("v", got), ("v", other), ("v", basis)],
-        [("v", (NVC, half), BF16)] * 3 + [("v", (2, NC * LANES, LANES // NV * count), BF16)],
+        [("h", (NVC, half), BF16)] * 3 + [("h", diagonals, BF16)],
         [
             pltpu.VMEM((2, 2, NV, NR // 2), F32),
             pltpu.VMEM((2, 2, NV, NR // 2), F32),
@@ -346,6 +386,11 @@
             pltpu.VMEM((NVC, NR // 2), BF16),
             pltpu.VMEM((half // LANES, NVC, LANES), F32),
             pltpu.VMEM((2, NVC, LANES), F32),
+            pltpu.VMEM((NVC, half), BF16),
+            pltpu.VMEM((NVC, half), BF16),
+            pltpu.VMEM((NVC, half), BF16),
+            pltpu.VMEM(diagonals, BF16),
+            pltpu.SemaphoreType.DMA((5,)),
         ],
         flops=2 * NVC * NR * half,
     )
@@ -353,13 +398,18 @@
     partial = call(
         apply_kernel,
         "apply",
-        [("v", valence), ("v", screen_got), ("v", conduction), ("v", swapped), ("v", diagonal)],
-        [("b", (pair_count, strips * groups, 2, share, states) if aligned else (2, count, NVC), BF16)],
+        [("h", valence), ("v", screen_got), ("h", conduction), ("h", swapped), ("h", diagonal)],
+        [("v", (pair_count, strips * groups, 2, share, states) if aligned else (2, count, NVC), BF16)],
         [
             pltpu.VMEM((half, half), BF16),
             pltpu.VMEM((half // LANES, NVC, LANES), F32),
             pltpu.VMEM((2, NVC, half), BF16),
             pltpu.VMEM((2, NVC // LANES * NC, NC * LANES), BF16),
+            pltpu.VMEM((NVC, half), BF16),
+            pltpu.VMEM((NVC, half), BF16),
+            pltpu.VMEM((NVC, half), BF16),
+            pltpu.VMEM(diagonals, BF16),
+            pltpu.SemaphoreType.DMA((5,)),
         ],
         flops=2 * NVC * half * half + 8 * NVC * NVC * half,
     )[0]

time: 79.1 us -> 62.7 us (0.79)
  local copies, waits for them, and re-layouts: 13.2 us -> 0 us
  Pallas kernels: 31.1 us -> 26.9 us
  waiting for transfers between devices: 7.75 us -> 8.92 us
    unnamed x24 -> x0, local copies, waits for them, and re-layouts: 13.2 us -> none
    pallas_call x5, Pallas kernels: 31.1 us -> 26.9 us  [call(): pl.pallas_call(body, out_shape=shapes, in_specs=specs, out_specs=out_spec...]
    all_to_all x1, waiting for transfers between devices: 6.04 us -> 7.21 us  [on_device(): lax.all_to_all(send, pair_axes, split_axis=0, concat_axis=0, tiled=True)]
  transfers between devices with their start and end apart: 3 -> 3, of which waited for: 2 -> 2; matrix products, arithmetic and copies ran while one was open for 0% -> 0% of each run, Pallas kernels for 12% -> 21%
where the time goes in v3:
time: 62.7 us; the launch traced here: 62.2 us
  Pallas kernels  26.9 us (43%)
  blocking collectives  15.3 us (24%)
  starting transfers between devices  11.1 us (18%)
  waiting for transfers between devices  8.92 us (14%)
    pallas_call x5, Pallas kernels, call(): pl.pallas_call(body, out_shape=shapes, in_specs=specs, out_specs=out_spec...  26.9 us
    all_to_all x1, blocking collectives, on_device(): lax.all_to_all(out_send, all_axes, split_axis=0, concat_axis=0, tiled=True)  15.3 us
    all_to_all x1, starting transfers between devices, on_device(): lax.all_to_all(send, pair_axes, split_axis=0, concat_axis=0, tiled=True)  7.32 us
    all_to_all x1, waiting for transfers between devices, on_device(): lax.all_to_all(send, pair_axes, split_axis=0, concat_axis=0, tiled=True)  7.21 us
    all_to_all x1, starting transfers between devices, on_device(): lax.all_to_all(screen_send, ('pl', 'bx'), split_axis=0, concat_axis=0, ti...  3.67 us
    ppermute x1, waiting for transfers between devices, on_device(): other = lax.ppermute(got, 'bc', [(i, i ^ 1) for i in range(groups)])  1.71 us
  transfers between devices with their start and end apart: 3, of which 2 were waited for; matrix products, arithmetic and copies ran while one was open for 0% of the time, Pallas kernels for 21%

profile of v3, /device:TPU:0, one launch (start us, length us, event | category | flops | bytes accessed | tf_op | source)
XLA Modules:
  0.0 62.2 jit_solution(13909476002202927763)
XLA Ops:
  0.0 2.7 %pack.1 = bf16[8,64,384]{2,1,0:T(8,128)(2,1)} custom-call(s32[2,8]{1,0:T(2,128)} %bitcast.12, bf16[23,64,256]{2,1,0:T(8,128)(2,1)} %bitcast.9, bf16[23,64,128]{2,1,0:T(8,128)(2,1)} %bitcast.11), custom_call_target="tpu_custom_call" | custom-call | bytes 1048576 | tf_op jit(solution)/shard_map/pack/pallas_call | solution.py:46
  2.7 7.3 %all-to-all-start = ((bf16[8,64,384]{2,1,0:T(8,128)(2,1)}), bf16[8,64,384]{2,1,0:T(8,128)(2,1)S(1)}, u32[]{:S(2)}, u32[]{:S(2)}) async-start(bf16[8,64,384]{2,1,0:T(8,128)(2,1)} %pack.1), calls=%async_computation | async-start | bytes 786432 | tf_op jit(solution)/shard_map/all_to_all | solution.py:360
  10.0 4.4 %prepare.1 = (bf16[1024,1024]{1,0:T(8,128)(2,1)S(1)}, bf16[8,128,256]{2,1,0:T(8,128)(2,1)}) custom-call(s32[8]{0:T(128)} %q_ref.1, bf16[1024,256]{1,0:T(8,128)(2,1)} %bitcast.10), custom_call_target="tpu_custom_call" | custom-call | flops 8388608 | bytes 1048576 | tf_op jit(solution)/shard_map/prepare/pallas_call | solution.py:46
  14.5 7.2 %all-to-all-done.own_ref = bf16[8,64,384]{2,1,0:T(8,128)(2,1)S(1)} async-done(((bf16[8,64,384]{2,1,0:T(8,128)(2,1)}), bf16[8,64,384]{2,1,0:T(8,128)(2,1)S(1)}, u32[]{:S(2)}, u32[]{:S(2)}) %all-to-all-start) | async-done | bytes 393248 | tf_op jit(solution)/shard_map/all_to_all | solution.py:360
  21.7 3.7 %all-to-all-start.1 = ((bf16[8,128,256]{2,1,0:T(8,128)(2,1)}), bf16[8,128,256]{2,1,0:T(8,128)(2,1)S(1)}, u32[]{:S(2)}, u32[]{:S(2)}) async-start(bf16[8,128,256]{2,1,0:T(8,128)(2,1)} %get-tuple-element.13), calls=%async_computation.1 | async-start | bytes 1048576 | tf_op jit(solution)/shard_map/all_to_all | solution.py:361
  25.4 0.1 collective-permute-start
  25.4 1.7 %collective-permute-done.other_ref = bf16[8,64,384]{2,1,0:T(8,128)(2,1)S(1)} collective-permute-done((bf16[8,64,384]{2,1,0:T(8,128)(2,1)S(1)}, bf16[8,64,384]{2,1,0:T(8,128)(2,1)S(1)}, u32[]{:S(2)}, u32[]{:S(2)}) %collective-permute-start) | collective-permute-done | bytes 393248 | tf_op jit(solution)/shard_map/ppermute | solution.py:362
  27.1 8.5 %transform.1 = (bf16[1024,512]{1,0:T(8,128)(2,1)}, bf16[1024,512]{1,0:T(8,128)(2,1)}, bf16[1024,512]{1,0:T(8,128)(2,1)}, bf16[2,4096,256]{2,1,0:T(8,128)(2,1)}) custom-call(bf16[8,64,384]{2,1,0:T(8,128)(2,1)S(1)} %all-to-all-done.own_ref, bf16[8,64,384]{2,1,0:T(8,128)(2,1)S(1)} %collective-permute-done.other_ref, ...), custom_call_target="tpu_custom_call" | custom-call | flops 2147483648 | bytes 1048576 | tf_op jit(solution)/shard_map/transform/pallas_call | solution.py:46
  35.6 0.0 all-to-all-done.1.screen_ref
  35.6 9.8 %apply.1 = bf16[8,4,2,16,128]{4,3,2,1,0:T(8,128)(2,1)S(1)} custom-call(bf16[1024,512]{1,0:T(8,128)(2,1)} %get-tuple-element.12.val_ref, bf16[8,128,256]{2,1,0:T(8,128)(2,1)S(1)} %all-to-all-done.1.screen_ref, bf16[1024,512]{1,0:T(8,128)(2,1)} %get-tuple-element.14.cond_ref, bf16[1024,512]{1,0:T(8,128)(2,1)} %get-tuple-element.15.swap_ref, ...), custom_call_target="tpu_custom_call" | custom-call | flops 4831838208 | bytes 1048576 | tf_op jit(solution)/shard_map/apply/pallas_call | solution.py:46
  45.5 15.3 %all_to_all.15 = bf16[32,2,16,128]{3,2,1,0:T(8,128)(2,1)S(1)} all-to-all(bf16[32,2,16,128]{3,2,1,0:T(8,128)(2,1)S(1)} %bitcast.8), channel_id=1, replica_groups=mesh['ph'=2,'pl'=4,'bx'=2,'bc'=2] {'ph','pl','bx','bc'}, dimensions={0} | all-to-all | bytes 524288 | tf_op jit(solution)/shard_map/all_to_all | solution.py:419
  60.8 1.4 %gather.1 = f32[23,16,128]{2,1,0:T(8,128)} custom-call(s32[2,8]{1,0:T(2,128)} %bitcast.13, bf16[2,4,2,2,2,16,128]{6,5,4,3,2,1,0:T(8,128)(2,1)S(1)} %bitcast.7), custom_call_target="tpu_custom_call" | custom-call | bytes 1048576 | tf_op jit(solution)/shard_map/gather/pallas_call | solution.py:46
Async XLA Ops:
  2.7 19.0 %all-to-all-start = ((bf16[8,64,384]{2,1,0:T(8,128)(2,1)}), bf16[8,64,384]{2,1,0:T(8,128)(2,1)S(1)}, u32[]{:S(2)}, u32[]{:S(2)}) async-start(bf16[8,64,384]{2,1,0:T(8,128)(2,1)} %pack.1), calls=%async_computation | async-start | bytes 786432 | tf_op jit(solution)/shard_map/all_to_all | solution.py:360
  21.7 13.9 %all-to-all-start.1 = ((bf16[8,128,256]{2,1,0:T(8,128)(2,1)}), bf16[8,128,256]{2,1,0:T(8,128)(2,1)S(1)}, u32[]{:S(2)}, u32[]{:S(2)}) async-start(bf16[8,128,256]{2,1,0:T(8,128)(2,1)} %get-tuple-element.13), calls=%async_computation.1 | async-start | bytes 1048576 | tf_op jit(solution)/shard_map/all_to_all | solution.py:361
  25.4 1.8 %collective-permute-start = (bf16[8,64,384]{2,1,0:T(8,128)(2,1)S(1)}, bf16[8,64,384]{2,1,0:T(8,128)(2,1)S(1)}, u32[]{:S(2)}, u32[]{:S(2)}) collective-permute-start(bf16[8,64,384]{2,1,0:T(8,128)(2,1)S(1)} %all-to-all-done.own_ref), channel_id=1, source_target_pairs={{0,1},{1,0},{2,3},{3,2},{4,5},{5,4},{6,7},{7,6},{8,9},{9,8},{10,11... | collective-permute-start | bytes 1179656 | tf_op jit(solution)/shard_map/ppermute | solution.py:362
